TPU v7x, 128 devices: a whole 4x4x4 slice. The times are simulated.
128 devices in a mesh: gx: 16 (over x, y), gy: 8 (over z, core).
Axes of the slice: x: 4, y: 4, z: 4, core: 2. Of those that a mesh axis runs over, the one named last changes fastest.
Arguments:
- state_in: float32 [4, 32768, 16, 128], P(None, ('gx', 'gy')), may hold values from -6 to 6
- stiffness: float32 [16, 16, 32768], P(None, None, ('gx', 'gy')), may hold values from -1.5 to 1.5
- elem_cell: int32 [32768], P(('gx', 'gy')), may hold values from 0 to 32767, as said below
- group_column: int32 [131072], P(('gx', 'gy')), may hold values from 0 to 131071, as said below
- group_inverse: bfloat16 [8192, 128, 128], P(('gx', 'gy')), may hold values from 0 to 0.875
Outputs:
- state_out: float32 [4, 32768, 16, 128], P(None, ('gx', 'gy'))
Inputs may be any that keep to these rules, and one draw needn't show every extreme that they name: `elem_cell`: device i * 8 + j (index i along gx, j along gy) holds in its 256 slots, in some order, exactly the cells with x from i * 16 to (i + 1) * 16 - 1 and y from j * 16 to (j + 1) * 16 - 1; every cell is held once. `group_column`: every column is named once. Column c lies on device c // 1024, slot p on device p // 1024; the 1024 slots of each device name exactly 8 columns of each device.
All inputs are finite; a program needn't handle non-finite values.
Results may differ from a plain program's by a relative error of at most 0.0031.
Values may be sent and summed in bfloat16 or wider, within the bound.
A program may use at most 128 MiB of HBM per device.

v0:
```python
import math

import jax
import jax.numpy as jnp
from jax import lax
from jax.sharding import PartitionSpec as P

GROUP_COLS = 16
EXD = 16
EYD = 16


exact_mode = lax.Precision.HIGHEST


def padded_2(block, sides, width):
    for axis, dim in sides:
        count = lax.axis_size(axis)
        forward = [(i, i + 1) for i in range(count - 1)]
        forward.append((count - 1, 0))
        backward = [(target, source) for source, target in forward]
        low = lax.ppermute(
            lax.slice_in_dim(block, block.shape[dim] - width, None, axis=dim), axis, forward
        )
        high = lax.ppermute(lax.slice_in_dim(block, 0, width, axis=dim), axis, backward)
        block = jnp.concatenate([low, block, high], axis=dim)
    return block


def lagrange_value(node_index, position, gll_nodes):
    running = 1.0
    for other_index in range(4):
        if other_index != node_index:
            running = (
                running
                * (position - gll_nodes[other_index])
                / (gll_nodes[node_index] - gll_nodes[other_index])
            )
    return running


def half_tables():
    gll_nodes = [-1.0, -1.0 / math.sqrt(5.0), 1.0 / math.sqrt(5.0), 1.0]
    halves = [[0.0] * 4, [0.0] * 4]
    for half_index, bounds in enumerate(((-1.0, 0.0), (0.0, 1.0))):
        lower_end, upper_end = bounds
        centre_point = 0.5 * (lower_end + upper_end)
        offset_gauss = 0.5 * (upper_end - lower_end) / math.sqrt(3.0)
        for node_index in range(4):
            first_value = lagrange_value(node_index, centre_point - offset_gauss, gll_nodes)
            second_value = lagrange_value(node_index, centre_point + offset_gauss, gll_nodes)
            halves[half_index][node_index] = (
                0.5 * (upper_end - lower_end) * (first_value + second_value)
            )
    product = [
        [
            sum((halves[row_index][k_index] * halves[col_index][k_index] for k_index in range(4)))
            for col_index in range(2)
        ]
        for row_index in range(2)
    ]
    determinant = product[0][0] * product[1][1] - product[0][1] * product[1][0]
    inverse = [
        [product[1][1] / determinant, -product[0][1] / determinant],
        [-product[1][0] / determinant, product[0][0] / determinant],
    ]
    spread = [
        [
            sum((halves[k_index][node_index] * inverse[k_index][col_index] for k_index in range(2)))
            for col_index in range(2)
        ]
        for node_index in range(4)
    ]
    return (jnp.asarray(halves, jnp.float32), jnp.asarray(spread, jnp.float32))


def add_shared(padded, axis_dim):
    interior = padded.shape[axis_dim] - 2
    middle = lax.slice_in_dim(padded, 1, interior + 1, axis=axis_dim)
    preceding = lax.slice_in_dim(padded, 0, interior, axis=axis_dim)
    following = lax.slice_in_dim(padded, 2, interior + 2, axis=axis_dim)
    layout = [1] * padded.ndim
    layout[axis_dim] = interior
    position = (jnp.arange(interior) % 4).reshape(layout)
    return (
        middle + jnp.where(position == 0, preceding, 0.0) + jnp.where(position == 3, following, 0.0)
    )


def sharing_count(rows_count, cols_count):
    along_x = jnp.where(jnp.arange(rows_count) % 4 % 3 == 0, 2.0, 1.0).astype(jnp.float32)
    along_y = jnp.where(jnp.arange(cols_count) % 4 % 3 == 0, 2.0, 1.0).astype(jnp.float32)
    return (along_x[:, None] * along_y[None, :])[:, :, None]


def assemble(tile_view):
    padded = padded_2(tile_view, (("gx", 1), ("gy", 2)), 1)
    summed = add_shared(add_shared(padded, 1), 2)
    return summed / sharing_count(summed.shape[1], summed.shape[2])


def regroup(blocks):
    return lax.all_to_all(blocks, ("gx", "gy"), split_axis=1, concat_axis=1, tiled=True)


def per_device(state_in, stiffness, elem_cell, group_column, group_inverse):
    fields = state_in.shape[0]
    elements = state_in.shape[1]
    levels = state_in.shape[3]
    devices = lax.axis_size("gx") * lax.axis_size("gy")
    columns_dev = 4 * elements
    per_peer = columns_dev // devices
    span_y = EYD * lax.axis_size("gy")
    tile_of_slot = elem_cell // span_y % EXD * EYD + elem_cell % span_y % EYD
    slot_of_tile = (
        jnp.zeros((elements,), jnp.int32)
        .at[tile_of_slot]
        .set(jnp.arange(elements, dtype=jnp.int32))
    )
    halves, spread = half_tables()
    tile_x = jnp.arange(EXD, dtype=jnp.int32)[:, None, None, None]
    node_a = jnp.arange(4, dtype=jnp.int32)[None, :, None, None]
    tile_y = jnp.arange(EYD, dtype=jnp.int32)[None, None, :, None]
    node_b = jnp.arange(4, dtype=jnp.int32)[None, None, None, :]
    node_order = (slot_of_tile[tile_x * EYD + tile_y] * 16 + 4 * node_a + node_b).reshape(-1)
    slot_order = (
        jnp.zeros((elements * 16,), jnp.int32)
        .at[node_order]
        .set(jnp.arange(elements * 16, dtype=jnp.int32))
    )
    local_term = jnp.einsum("nme,feml->fenl", stiffness, state_in, precision=exact_mode)
    combined = (state_in + local_term).reshape(fields, elements * 16, levels)
    tile_view = jnp.take(combined, node_order, axis=1).reshape(fields, 4 * EXD, 4 * EYD, levels)
    dynamics = assemble(tile_view)
    split_nodes = dynamics.reshape(fields, EXD, 4, EYD, 4, levels)
    columns = jnp.einsum("ia,jb,fxaybl->fxyijl", halves, halves, split_nodes, precision=exact_mode)
    columns = columns.astype(jnp.bfloat16).reshape(fields, columns_dev, levels)
    source = group_column // columns_dev
    by_source = jnp.argsort(source, stable=True)
    wanted = (group_column % columns_dev)[by_source].reshape(devices, per_peer)
    requested = lax.all_to_all(
        wanted, ("gx", "gy"), split_axis=0, concat_axis=0, tiled=True
    ).reshape(-1)
    tile_column = tile_of_slot[requested // 4] * 4 + requested % 4
    outgoing = columns[:, tile_column].reshape(fields, devices, per_peer, levels)
    incoming = regroup(outgoing).reshape(fields, columns_dev, levels)
    placing = (
        jnp.zeros((columns_dev,), jnp.int32)
        .at[by_source]
        .set(jnp.arange(columns_dev, dtype=jnp.int32))
    )
    physics = incoming[:, placing].reshape(fields, columns_dev // GROUP_COLS, GROUP_COLS, levels)
    smoothed = jnp.einsum(
        "gkl,fgjl->fgjk", group_inverse, physics, preferred_element_type=jnp.float32
    )
    tendency = (
        (smoothed - physics.astype(jnp.float32))
        .astype(jnp.bfloat16)
        .reshape(fields, columns_dev, levels)
    )
    returning = tendency[:, by_source].reshape(fields, devices, per_peer, levels)
    received = regroup(returning).reshape(fields, columns_dev, levels)
    unpack = (
        jnp.zeros((columns_dev,), jnp.int32)
        .at[tile_column]
        .set(jnp.arange(columns_dev, dtype=jnp.int32))
    )
    back_columns = received[:, unpack].reshape(fields, EXD, EYD, 2, 2, levels).astype(jnp.float32)
    on_nodes = jnp.einsum(
        "ai,bj,fxyijl->fxaybl", spread, spread, back_columns, precision=exact_mode
    )
    updated = dynamics + assemble(on_nodes.reshape(fields, 4 * EXD, 4 * EYD, levels))
    updated = updated.reshape(fields, elements * 16, levels)
    return jnp.take(updated, slot_order, axis=1).reshape(fields, elements, 16, levels)


def solution(mesh):
    placed = (
        P(None, ("gx", "gy"), None, None),
        P(None, None, ("gx", "gy")),
        P(("gx", "gy")),
        P(("gx", "gy")),
        P(("gx", "gy"), None, None),
    )
    return jax.shard_map(
        per_device,
        mesh=mesh,
        in_specs=placed,
        out_specs=P(None, ("gx", "gy"), None, None),
        check_vma=False,
    )
```

profile of v0, /device:TPU:1, one launch (start us, length us, event | category | flops | bytes accessed | tf_op | source)
XLA Modules:
  0.0 415.0 jit_solution(11420030684421999415)
XLA Ops:
  1.0 4.4 %sort.17 = (s32[1024]{0:T(1024)}, s32[1024]{0:T(1024)S(1)}) sort(s32[1024]{0:T(1024)S(1)} %get-tuple-element.20, s32[1024]{0:T(1024)S(1)} %iota.81), dimensions={0}, to_apply=%region_1.3 | sort | flops 10240 | bytes 16384 | tf_op jit(solution)/shard_map/jit(argsort)/sort | solution.py:139
  5.4 4.5 %gather_fusion.1 = s32[1024]{0:T(1024)S(1)} fusion(s32[1024]{0:T(1024)S(1)} %get-tuple-element.21, s32[1024]{0:T(1024)S(1)} %get-tuple-element.19), kind=kCustom, calls=%fused_computation.3 | custom fusion | bytes 12288 | tf_op jit(solution)/shard_map/gather | solution.py:140
  10.6 11.5 %all-to-all-start = ((s32[128,1,8]{2,1,0:T(1,128)}), s32[128,1,8]{2,1,0:T(1,128)S(1)}, u32[]{:S(2)}, u32[]{:S(2)}) async-start(s32[128,1,8]{2,1,0:T(1,128)} %bitcast.12), calls=%async_computation | async-start | bytes 131072 | tf_op jit(solution)/shard_map/all_to_all | solution.py:141
  29.5 16.1 %bitcast_add_fusion = f32[4,256,16,128]{3,2,0,1:T(8,128)S(1)} fusion(f32[4,256,16,128]{3,2,1,0:T(8,128)} %param.9, f32[16,16,256,1]{1,0,3,2:T(8,128)} %copy.50), kind=kOutput, calls=%fused_computation.34 | convolution fusion | flops 404750336 | bytes 17039360 | tf_op jit(solution)/shard_map/nme,feml->fenl/dot_general | solution.py:131
  46.5 18.6 %copy.32 = f32[4,4096,128]{2,0,1:T(4,128)} copy(f32[4,4096,128]{2,1,0:T(8,128)S(1)} %bitcast.80) | data formatting | bytes 16777216 | tf_op jit(solution)/shard_map/reshape | solution.py:132
  65.1 33.6 %gather_fusion.7 = f32[4096,4,128]{2,1,0:T(4,128)} fusion(f32[4,4096,128]{2,0,1:T(4,128)} %copy.32, s32[4096]{0:T(1024)S(1)} %fusion.31), kind=kCustom, calls=%fused_computation.clone | custom fusion | bytes 16793600 | tf_op jit(solution)/shard_map/jit(_take)/gather | solution.py:133
  98.7 16.8 %broadcast_select_fusion.1 = f32[4096,4,128]{2,1,0:T(4,128)S(1)} fusion(f32[4096,4,128]{2,1,0:T(4,128)} %gather_fusion.7, pred[4096]{0:T(1024)(128)(4,1)S(1)} %compare_and_fusion.1), kind=kLoop, calls=%fused_computation.44 | loop fusion | flops 2097152 | bytes 16781312 | tf_op jit(solution)/shard_map/jit(_take)/select_n | solution.py:133
  125.4 6.8 %gather_fusion.2 = s32[1024]{0:T(1024)S(1)} fusion(s32[256]{0:T(256)S(1)} %get-tuple-element.9, s32[1024]{0:T(1024)S(1)} %broadcast_clamp_fusion.2), kind=kCustom, calls=%fused_computation.4 | custom fusion | bytes 12288 | tf_op jit(solution)/shard_map/gather | solution.py:144
  132.3 4.6 %constant_dynamic-update-slice_fusion.1 = f32[4,66,64,128]{3,2,1,0:T(8,128)S(1)} fusion(f32[4,66,64,128]{3,2,1,0:T(8,128)S(1)} %constant_dynamic-update-slice_fusion.2, f32[4,64,64,128]{3,0,2,1:T(4,128)} %bitcast.77), kind=kLoop, calls=%fused_computation.80 | loop fusion | bytes 16777216
  143.9 5.2 %pad_maximum_fusion = f32[4,66,66,128]{3,2,1,0:T(8,128)} fusion(f32[4,66,1,128]{3,2,1,0:T(1,128)S(1)} %collective-permute-done.3, f32[4,66,64,128]{3,2,1,0:T(8,128)S(1)} %constant_dynamic-update-slice_fusion, f32[4,66,1,128]{3,2,1,0:T(1,128)S(1)} %collective-permute-done.2), kind=kLoop, calls=%fused_computation.13 | loop fusion | flops 4460544 | bytes 17842176 | tf_op jit(solution)/shard_map/concatenate | solution.py:26
  149.2 10.4 %fusion.2 = f32[4,64,66,128]{3,2,1,0:T(8,128)S(1)} fusion(f32[4,66,66,128]{3,2,1,0:T(8,128)} %pad_maximum_fusion, pred[64]{0:T(512)(128)(4,1)S(1)} %get-tuple-element.24, pred[64]{0:T(512)(128)(4,1)S(1)} %get-tuple-element.23), kind=kLoop, calls=%fused_computation.20 | loop fusion | flops 8650752 | bytes 34603136 | tf_op jit(solution)/shard_map/add | solution.py:86
  159.6 6.3 %fusion.9 = f32[4,64,64,128]{3,2,1,0:T(8,128)} fusion(f32[4,64,66,128]{3,2,1,0:T(8,128)S(1)} %fusion.2, f32[64,64]{1,0:T(8,128)S(1)} %broadcast_multiply_fusion, pred[64]{0:T(512)(128)(4,1)S(1)} %get-tuple-element.24, pred[64]{0:T(512)(128)(4,1)S(1)} %get-tuple-element.23), kind=kLoop, calls=%fused_computation.31 | loop fusion | flops 10485760 | bytes 33570944 | tf_op jit(solution)/shard_map/div | solution.py:99
  165.9 23.0 %fusion.11 = f32[4,16,16,4,128,2]{4,5,3,2,1,0:T(2,128)S(1)} fusion(f32[2,4,1,1,1,1]{1,0,5,4,3,2:T(2,128)S(1)} %copy-done.7, f32[4,16,4,16,4,128]{5,4,3,2,1,0:T(4,128)} %bitcast.81), kind=kOutput, calls=%fused_computation.35 | convolution fusion | flops 50331648 | bytes 12582944 | tf_op jit(solution)/shard_map/ia,jb,fxaybl->fxyijl/dot_general | solution.py:136
  188.8 7.7 %fusion.25 = bf16[4,16,16,128,2,2]{3,5,4,2,1,0:T(2,128)(2,1)S(1)} fusion(f32[2,4,1,1,1,1]{1,0,5,4,3,2:T(2,128)S(1)} %copy-done.7, f32[4,16,16,4,128,2]{4,5,3,2,1,0:T(2,128)S(1)} %fusion.11), kind=kOutput, calls=%fused_computation.49 | convolution fusion | flops 25690112 | bytes 5242912 | tf_op jit(solution)/shard_map/ia,jb,fxaybl->fxyijl/dot_general | solution.py:136
  198.3 8.8 %gather_fusion.3 = bf16[1024,4,128]{2,1,0:T(4,128)(2,1)} fusion(bf16[4,1024,128]{2,0,1:T(4,128)(2,1)} %copy.39, s32[1024]{0:T(1024)S(1)} %broadcast_clamp_fusion), kind=kCustom, calls=%fused_computation.5 | custom fusion | bytes 2101248 | tf_op jit(solution)/shard_map/gather | solution.py:145
  207.1 6.2 %all-to-all-start.1 = ((bf16[4,128,8,128]{3,0,2,1:T(4,128)(2,1)}), bf16[4,128,8,128]{3,0,2,1:T(4,128)(2,1)}, u32[]{:S(2)}, u32[]{:S(2)}) async-start(bf16[4,128,8,128]{3,0,2,1:T(4,128)(2,1)} %bitcast.85), calls=%async_computation.1 | async-start | bytes 2097152 | tf_op jit(solution)/shard_map/all_to_all | solution.py:103
  213.6 4.3 %scatter_custom_fusion.1 = s32[1024]{0:T(1024)S(1)} fusion(s32[1024]{0:T(1024)S(1)} %get-tuple-element.18, s32[1024]{0:T(1024)S(1)} %iota.82, s32[]{:T(128)} %constant.166.clone.1), kind=kCustom, calls=%fused_computation.105 | custom fusion | bytes 4100 | tf_op jit(solution)/shard_map/scatter | solution.py:150
  217.9 14.2 %all-to-all-done.1 = bf16[4,128,8,128]{3,0,2,1:T(4,128)(2,1)} async-done(((bf16[4,128,8,128]{3,0,2,1:T(4,128)(2,1)}), bf16[4,128,8,128]{3,0,2,1:T(4,128)(2,1)}, u32[]{:S(2)}, u32[]{:S(2)}) %all-to-all-start.1) | async-done | bytes 1048608 | tf_op jit(solution)/shard_map/all_to_all | solution.py:103
  232.2 4.8 %gather_fusion.4 = bf16[1024,4,128]{2,1,0:T(4,128)(2,1)S(1)} fusion(bf16[4,1024,128]{2,0,1:T(4,128)(2,1)} %bitcast.18, s32[1024]{0:T(1024)S(1)} %fusion.36), kind=kCustom, calls=%fused_computation.6 | custom fusion | bytes 2101248 | tf_op jit(solution)/shard_map/gather | solution.py:152
  239.7 7.6 %gather_fusion.5 = bf16[1024,4,128]{2,1,0:T(4,128)(2,1)} fusion(bf16[4,1024,128]{2,0,1:T(4,128)(2,1)S(1)} %copy.44, s32[1024]{0:T(1024)S(1)} %get-tuple-element.19), kind=kCustom, calls=%fused_computation.7 | custom fusion | bytes 2101248 | tf_op jit(solution)/shard_map/gather | solution.py:161
  247.3 4.6 %all-to-all-start.2 = ((bf16[4,128,8,128]{3,0,2,1:T(4,128)(2,1)}), bf16[4,128,8,128]{3,0,2,1:T(4,128)(2,1)S(1)}, u32[]{:S(2)}, u32[]{:S(2)}) async-start(bf16[4,128,8,128]{3,0,2,1:T(4,128)(2,1)} %bitcast.26), calls=%async_computation.2 | async-start | bytes 2097152 | tf_op jit(solution)/shard_map/all_to_all | solution.py:103
  251.9 15.5 %scatter_custom_fusion.3 = s32[4096]{0:T(1024)S(1)} fusion(s32[4096]{0:T(1024)S(1)} %bitcast.93, s32[4096]{0:T(1024)S(1)} %iota.84, s32[]{:T(128)} %constant.166.clone.1), kind=kCustom, calls=%fused_computation.77 | custom fusion | bytes 16388 | tf_op jit(solution)/shard_map/scatter | solution.py:129
  267.4 4.5 %scatter_custom_fusion.2 = s32[1024]{0:T(1024)S(1)} fusion(s32[1024]{0:T(1024)S(1)} %bitcast.91, s32[1024]{0:T(1024)S(1)} %iota.83, s32[]{:T(128)} %constant.166.clone.1), kind=kCustom, calls=%fused_computation.103 | custom fusion | bytes 4100 | tf_op jit(solution)/shard_map/scatter | solution.py:166
  275.6 3.7 fusion.28
  279.3 16.3 %convolution_bitcast_fusion = f32[4,16,4,16,4,128]{5,4,2,3,1,0:T(4,128)} fusion(f32[4,2,1,1,1,1]{0,1,5,4,3,2:T(2,128)S(1)} %copy-done.6, f32[4,16,16,2,128,4]{4,5,3,2,1,0:T(4,128)S(1)} %fusion.28), kind=kOutput, calls=%fused_computation.39 | convolution fusion | flops 50331648 | bytes 12582944 | tf_op jit(solution)/shard_map/ai,bj,fxyijl->fxaybl/dot_general | solution.py:169
  295.7 9.0 %copy.47 = f32[4,16,4,16,4,128]{5,4,3,2,1,0:T(4,128)} copy(f32[4,16,4,16,4,128]{5,4,2,3,1,0:T(4,128)} %convolution_bitcast_fusion) | data formatting | bytes 16777216 | tf_op jit(solution)/shard_map/ai,bj,fxyijl->fxaybl/transpose | solution.py:169
  326.6 5.3 %fusion = f32[4,64,66,128]{3,2,1,0:T(8,128)} fusion(f32[4,66,66,128]{3,2,1,0:T(8,128)S(1)} %pad_maximum_fusion.1, pred[64]{0:T(512)(128)(4,1)S(1)} %get-tuple-element.24, pred[64]{0:T(512)(128)(4,1)S(1)} %get-tuple-element.23), kind=kLoop, calls=%fused_computation.16 | loop fusion | flops 8650752 | bytes 34603136 | tf_op jit(solution)/shard_map/add | solution.py:86
  331.9 14.2 %fusion.6 = f32[4,64,64,128]{3,2,1,0:T(8,128)} fusion(f32[4,64,66,128]{3,2,1,0:T(8,128)} %fusion, f32[64,64]{1,0:T(8,128)S(1)} %broadcast_multiply_fusion, pred[64]{0:T(512)(128)(4,1)S(1)} %get-tuple-element.24, pred[64]{0:T(512)(128)(4,1)S(1)} %get-tuple-element.23, f32[4,64,66,128]{3,2,1,0:T(8,128)S(1)} %bitcast.72), kind=kLoop, calls=%fused_computation.26 | loop fusion | flops 23068672 | bytes 58736768 | tf_op jit(solution)/shard_map/add | solution.py:172
  346.1 14.6 %copy.48 = f32[4,64,64,128]{3,0,2,1:T(4,128)} copy(f32[4,64,64,128]{3,2,1,0:T(8,128)} %fusion.6) | data formatting | bytes 16777216 | tf_op jit(solution)/shard_map/add | solution.py:172
  360.7 33.4 %gather_fusion.8 = f32[4096,4,128]{2,1,0:T(4,128)} fusion(f32[4,4096,128]{2,0,1:T(4,128)} %bitcast.78, s32[4096]{0:T(1024)S(1)} %fusion.32), kind=kCustom, calls=%fused_computation.1.clone | custom fusion | bytes 16793600 | tf_op jit(solution)/shard_map/jit(_take)/gather | solution.py:174
  394.1 16.4 %broadcast_select_fusion = f32[4096,4,128]{2,1,0:T(4,128)S(1)} fusion(f32[4096,4,128]{2,1,0:T(4,128)} %gather_fusion.8, pred[4096]{0:T(1024)(128)(4,1)S(1)} %compare_and_fusion), kind=kLoop, calls=%fused_computation.43 | loop fusion | flops 2097152 | bytes 16781312 | tf_op jit(solution)/shard_map/jit(_take)/select_n | solution.py:174
  410.5 4.1 copy.49
  (97 shorter events, 57.1 us)
Async XLA Ops:
  0.0 237.1 %copy-start = (bf16[64,128,128]{2,1,0:T(8,128)(2,1)S(1)}, bf16[64,128,128]{2,1,0:T(8,128)(2,1)}, u32[]{:S(2)}) copy-start(bf16[64,128,128]{2,1,0:T(8,128)(2,1)} %param.13) | copy-start | bytes 6291460
  0.0 27.1 %copy-start.5 = (f32[16,16,256]{2,1,0:T(8,128)S(1)}, f32[16,16,256]{2,1,0:T(8,128)}, u32[]{:S(2)}) copy-start(f32[16,16,256]{2,1,0:T(8,128)} %param.10) | copy-start | bytes 786436
  10.6 113.4 %all-to-all-start = ((s32[128,1,8]{2,1,0:T(1,128)}), s32[128,1,8]{2,1,0:T(1,128)S(1)}, u32[]{:S(2)}, u32[]{:S(2)}) async-start(s32[128,1,8]{2,1,0:T(1,128)} %bitcast.12), calls=%async_computation | async-start | bytes 131072 | tf_op jit(solution)/shard_map/all_to_all | solution.py:141
  115.5 3.4 copy-start.4
  119.0 13.3 %collective-permute-start = (f32[4,1,64,128]{3,2,1,0:T(8,128)S(1)}, f32[4,1,64,128]{3,2,1,0:T(8,128)S(1)}, u32[]{:S(2)}, u32[]{:S(2)}) collective-permute-start(f32[4,1,64,128]{3,2,1,0:T(8,128)S(1)} %copy.74), channel_id=1, source_target_pairs={{0,8},{8,16},{16,24},{24,32},{32,40},{40,48},{48,56},{56,64},{64,7... | collective-permute-start | bytes 393224 | tf_op jit(solution)/shard_map/ppermute | solution.py:22
  120.4 16.4 %collective-permute-start.1 = (f32[4,1,64,128]{3,2,1,0:T(8,128)S(1)}, f32[4,1,64,128]{3,2,1,0:T(8,128)S(1)}, u32[]{:S(2)}, u32[]{:S(2)}) collective-permute-start(f32[4,1,64,128]{3,2,1,0:T(8,128)S(1)} %copy.75), channel_id=1, source_target_pairs={{8,0},{16,8},{24,16},{32,24},{40,32},{48,40},{56,48},{64,56},{72,6... | collective-permute-start | bytes 393224 | tf_op jit(solution)/shard_map/ppermute | solution.py:25
  137.1 4.3 %collective-permute-start.2 = (f32[4,66,1,128]{3,2,1,0:T(1,128)S(1)}, f32[4,66,1,128]{3,2,1,0:T(1,128)S(1)}, u32[]{:S(2)}, u32[]{:S(2)}) collective-permute-start(f32[4,66,1,128]{3,2,1,0:T(1,128)S(1)} %get-tuple-element.12), channel_id=1, source_target_pairs={{0,1},{1,2},{2,3},{3,4},{4,5},{5,6},{6,7},{7,0},{8,9},{9,10},{10,1... | collective-permute-start | bytes 405512 | tf_op jit(solution)/shard_map/ppermute | solution.py:22
  139.4 4.6 %collective-permute-start.3 = (f32[4,66,1,128]{3,2,1,0:T(1,128)S(1)}, f32[4,66,1,128]{3,2,1,0:T(1,128)S(1)}, u32[]{:S(2)}, u32[]{:S(2)}) collective-permute-start(f32[4,66,1,128]{3,2,1,0:T(1,128)S(1)} %get-tuple-element.13), channel_id=1, source_target_pairs={{1,0},{2,1},{3,2},{4,3},{5,4},{6,5},{7,6},{0,7},{9,8},{10,9},{11,1... | collective-permute-start | bytes 405512 | tf_op jit(solution)/shard_map/ppermute | solution.py:25
  159.5 6.3 %copy-start.2 = (f32[4,64,66,128]{3,2,1,0:T(8,128)}, f32[4,64,66,128]{3,2,1,0:T(8,128)S(1)}, u32[]{:S(2)}) copy-start(f32[4,64,66,128]{3,2,1,0:T(8,128)S(1)} %fusion.2) | copy-start | bytes 25952260
  159.6 6.3 %copy-start.7 = (f32[2,4,1,1,1,1]{1,0,5,4,3,2:T(2,128)S(1)}, f32[2,4,1,1,1,1]{1,0,5,4,3,2:T(2,128)}, u32[]{:S(2)}) copy-start(f32[2,4,1,1,1,1]{1,0,5,4,3,2:T(2,128)} %constant.188) | copy-start | bytes 100
  207.1 25.1 %all-to-all-start.1 = ((bf16[4,128,8,128]{3,0,2,1:T(4,128)(2,1)}), bf16[4,128,8,128]{3,0,2,1:T(4,128)(2,1)}, u32[]{:S(2)}, u32[]{:S(2)}) async-start(bf16[4,128,8,128]{3,0,2,1:T(4,128)(2,1)} %bitcast.85), calls=%async_computation.1 | async-start | bytes 2097152 | tf_op jit(solution)/shard_map/all_to_all | solution.py:103
  236.9 38.6 %copy-start.6 = (f32[4,2,1,1,1,1]{0,1,5,4,3,2:T(2,128)S(1)}, f32[4,2,1,1,1,1]{0,1,5,4,3,2:T(2,128)}, u32[]{:S(2)}) copy-start(f32[4,2,1,1,1,1]{0,1,5,4,3,2:T(2,128)} %constant.189) | copy-start | bytes 100
  247.3 24.7 %all-to-all-start.2 = ((bf16[4,128,8,128]{3,0,2,1:T(4,128)(2,1)}), bf16[4,128,8,128]{3,0,2,1:T(4,128)(2,1)S(1)}, u32[]{:S(2)}, u32[]{:S(2)}) async-start(bf16[4,128,8,128]{3,0,2,1:T(4,128)(2,1)} %bitcast.26), calls=%async_computation.2 | async-start | bytes 2097152 | tf_op jit(solution)/shard_map/all_to_all | solution.py:103
  304.6 18.2 %copy-start.3 = (f32[4,16,4,16,4,128]{5,4,3,2,1,0:T(4,128)S(1)}, f32[4,16,4,16,4,128]{5,4,3,2,1,0:T(4,128)}, u32[]{:S(2)}) copy-start(f32[4,16,4,16,4,128]{5,4,3,2,1,0:T(4,128)} %copy.47) | copy-start | bytes 25165828
  305.8 7.4 %collective-permute-start.4 = (f32[4,1,64,128]{3,2,1,0:T(8,128)S(1)}, f32[4,1,64,128]{3,2,1,0:T(8,128)S(1)}, u32[]{:S(2)}, u32[]{:S(2)}) collective-permute-start(f32[4,1,64,128]{3,2,1,0:T(8,128)S(1)} %get-tuple-element.14), channel_id=1, source_target_pairs={{0,8},{8,16},{16,24},{24,32},{32,40},{40,48},{48,56},{56,64},{64,7... | collective-permute-start | bytes 393224 | tf_op jit(solution)/shard_map/ppermute | solution.py:22
  307.3 5.9 %collective-permute-start.5 = (f32[4,1,64,128]{3,2,1,0:T(8,128)S(1)}, f32[4,1,64,128]{3,2,1,0:T(8,128)S(1)}, u32[]{:S(2)}, u32[]{:S(2)}) collective-permute-start(f32[4,1,64,128]{3,2,1,0:T(8,128)S(1)} %get-tuple-element.15), channel_id=1, source_target_pairs={{8,0},{16,8},{24,16},{32,24},{40,32},{48,40},{56,48},{64,56},{72,6... | collective-permute-start | bytes 393224 | tf_op jit(solution)/shard_map/ppermute | solution.py:25
  314.9 5.5 %collective-permute-start.6 = (f32[4,66,1,128]{3,2,1,0:T(1,128)S(1)}, f32[4,66,1,128]{3,2,1,0:T(1,128)S(1)}, u32[]{:S(2)}, u32[]{:S(2)}) collective-permute-start(f32[4,66,1,128]{3,2,1,0:T(1,128)S(1)} %get-tuple-element.10), channel_id=1, source_target_pairs={{0,1},{1,2},{2,3},{3,4},{4,5},{5,6},{6,7},{7,0},{8,9},{9,10},{10,1... | collective-permute-start | bytes 405512 | tf_op jit(solution)/shard_map/ppermute | solution.py:22
  318.4 4.4 %collective-permute-start.7 = (f32[4,66,1,128]{3,2,1,0:T(1,128)S(1)}, f32[4,66,1,128]{3,2,1,0:T(1,128)S(1)}, u32[]{:S(2)}, u32[]{:S(2)}) collective-permute-start(f32[4,66,1,128]{3,2,1,0:T(1,128)S(1)} %get-tuple-element.11), channel_id=1, source_target_pairs={{1,0},{2,1},{3,2},{4,3},{5,4},{6,5},{7,6},{0,7},{9,8},{10,9},{11,1... | collective-permute-start | bytes 405512 | tf_op jit(solution)/shard_map/ppermute | solution.py:25
  322.9 9.0 %slice-start = ((s8[9437184]{0:T(1024)(128)(4,1)}), s8[4194304]{0:T(1024)(128)(4,1)S(1)}, s32[]{:S(2)}) async-start(s8[9437184]{0:T(1024)(128)(4,1)} %bitcast.71), calls=%async_computation.3 | async-start | bytes 8388608
  326.5 5.3 %slice-start.1 = ((s8[9437184]{0:T(1024)(128)(4,1)}), s8[4194304]{0:T(1024)(128)(4,1)S(1)}, s32[]{:S(2)}) async-start(s8[9437184]{0:T(1024)(128)(4,1)} %bitcast.71), calls=%async_computation.4 | async-start | bytes 8388608
  326.5 5.3 %slice-start.2 = ((s8[9437184]{0:T(1024)(128)(4,1)}), s8[1048576]{0:T(1024)(128)(4,1)S(1)}, s32[]{:S(2)}) async-start(s8[9437184]{0:T(1024)(128)(4,1)} %bitcast.71), calls=%async_computation.5 | async-start | bytes 2097152
  410.4 4.2 %copy-start.1 = (bf16[64,128,128]{2,1,0:T(8,128)(2,1)S(1)}, bf16[64,128,128]{2,1,0:T(8,128)(2,1)}, u32[]{:S(2)}) copy-start(bf16[64,128,128]{2,1,0:T(8,128)(2,1)} %param.13) | copy-start | bytes 6291460
where the time goes:
time: 418 us; the launch traced here: 415 us
  local copies, waits for them, and re-layouts  195 us (47%)
  other arithmetic  87.3 us (21%)
  matrix products  68.4 us (16%)
  starting transfers between devices  38.1 us (9%)
  waiting for transfers between devices  25.5 us (6%)
    gather x1, local copies, waits for them, and re-layouts, per_device(): jnp.take(combined, node_order, axis=1)  33.6 us
    gather x1, local copies, waits for them, and re-layouts, per_device(): jnp.take(updated, slot_order, axis=1).reshape(fields, elements, 16, levels)  33.4 us
    dot_general x2, matrix products, per_device(): jnp.einsum('ia,jb,fxaybl->fxyijl', halves, halves, split_nodes, precision...  30.6 us
    dot_general x2, matrix products, per_device(): jnp.einsum('ai,bj,fxyijl->fxaybl', spread, spread, back_columns, precisio...  20.1 us
    reshape x1, local copies, waits for them, and re-layouts, per_device(): combined = (state_in + local_term).reshape(fields, elements * 16, levels)  18.6 us
    select_n x1, other arithmetic, per_device(): jnp.take(combined, node_order, axis=1)  16.8 us
    select_n x1, other arithmetic, per_device(): jnp.take(updated, slot_order, axis=1).reshape(fields, elements, 16, levels)  16.4 us
    dot_general x1, matrix products, per_device(): jnp.einsum('nme,feml->fenl', stiffness, state_in, precision=exact_mode)  16.1 us
  transfers between devices with their start and end apart: 11, of which 6 were waited for; matrix products, arithmetic and copies ran while one was open for 32% of the time, Pallas kernels for 0%

commit v1 on v0

v1 whole, which is shorter than its diff:
```python
import functools
import math

import jax
import jax.numpy as jnp
import ml_dtypes
import numpy as np
from jax import lax
from jax.experimental import pallas as pl
from jax.experimental.pallas import tpu as pltpu
from jax.sharding import PartitionSpec as P

F32, BF16, I32 = jnp.float32, jnp.bfloat16, jnp.int32
MESH = pl.DeviceIdType.MESH
NX, NY = 16, 8
ND = NX * NY
TX = TY = 16
NE = TX * TY
NC = 4 * NE
LEV = 128
NH = 2
WEST, EAST, SOUTH, NORTH = 0, 18, 36, 52
NHALO = 68
RX = 80
RROWS = 18 * RX + 16
CORNERS = (
    (1, 1, 4, 15, 15, 15),
    (-1, 1, 5, 0, 15, 3),
    (1, -1, 6, 15, 0, 12),
    (-1, -1, 7, 0, 0, 0),
)


def lagrange_value(node, position, nodes):
    value = 1.0
    for other in range(4):
        if other != node:
            value *= (position - nodes[other]) / (nodes[node] - nodes[other])
    return value


def tables():
    nodes = [-1.0, -1.0 / math.sqrt(5.0), 1.0 / math.sqrt(5.0), 1.0]
    halves = np.zeros((2, 4))
    for i, (low, high) in enumerate(((-1.0, 0.0), (0.0, 1.0))):
        centre, offset = 0.5 * (low + high), 0.5 * (high - low) / math.sqrt(3.0)
        for a in range(4):
            halves[i, a] = (
                0.5
                * (high - low)
                * (
                    lagrange_value(a, centre - offset, nodes)
                    + lagrange_value(a, centre + offset, nodes)
                )
            )
    spread = halves.T @ np.linalg.inv(halves @ halves.T)
    return halves.astype(np.float32).astype(np.float64), spread.astype(np.float32).astype(np.float64)


def split_bf16(table):
    high = table.astype(ml_dtypes.bfloat16)
    low = (table - high.astype(np.float64)).astype(ml_dtypes.bfloat16)
    return high, low


def constant_tables():
    halves, spread = tables()
    cols = np.einsum("ia,jb,yz->iyjzab", halves, halves, np.eye(TY)).reshape(64, 256)
    col_high, col_low = split_bf16(cols)
    along = np.zeros((4, 3, 2))
    along[:, 1, :] = spread
    along[0, 0, :] += spread[3]
    along[3, 2, :] += spread[0]
    along[0] *= 0.5
    along[3] *= 0.5
    along_y = np.zeros((TY, 4, 40))
    for y in range(TY):
        for step in range(3):
            other = y + step - 1
            base = 32 if other < 0 else 34 if other >= TY else 2 * other
            along_y[y, :, base : base + 2] += along[:, step, :]
    update = np.zeros((256, 256))
    update[:, :240] = np.einsum("asi,ybr->yabsir", along, along_y).reshape(256, 240)
    up_high, up_low = split_bf16(update)
    return np.concatenate([col_high, col_low], 0), np.concatenate([up_high, up_low], 0)


def iota(shape, dim):
    return lax.broadcasted_iota(I32, shape, dim)


def dot(left, right):
    return jnp.dot(left, right, preferred_element_type=F32)


def dot_nt(left, right):
    return lax.dot_general(left, right, (((1,), (1,)), ((), ())), preferred_element_type=F32)


class Peers:
    def __init__(self, gx, gy):
        self.x, self.y = lax.div(gx, 4), lax.rem(gx, 4)
        self.z, self.core = lax.div(gy, 2), lax.rem(gy, 2)
        self.xs = [lax.rem(self.x + a, 4) * 4 for a in range(4)]
        self.zs = [lax.rem(self.z + d, 4) * 2 for d in range(4)]
        self.cores = [self.core, 1 - self.core]

    def block(self, b, with_self=False):
        ys = [lax.rem(self.y + b + a, 4) for a in range(4)]
        back_b = lax.rem(4 - b, 4) if not isinstance(b, int) else -b % 4
        found = []
        for d in range(4):
            for a in range(4):
                for c in range(2):
                    if isinstance(b, int) and b == d == a == c == 0 and not with_self:
                        continue
                    tgx = self.xs[a] + ys[a]
                    tgy = self.zs[(d + a) % 4] + self.cores[c]
                    inner = d * 8 + a * 2 + c
                    back = -d % 4 * 8 + -a % 4 * 2 + c
                    found.append((tgx, tgy, b * 32 + inner, back_b * 32 + back))
        return found

    def position(self, source):
        a = ((source >> 5) - self.x) & 3
        b = (((source >> 3) & 3) - self.y - a) & 3
        d = (((source >> 1) & 3) - self.z - a) & 3
        c = ((source & 1) - self.core) & 1
        return b * 32 + d * 8 + a * 2 + c


def combine_kernel(cell_ref, state_hbm, stiff_hbm, out_ref, st, xs, w, stiff_sem, state_sem):
    stiff_copy = pltpu.make_async_copy(stiff_hbm, xs, stiff_sem)
    stiff_copy.start()
    loads = []
    for part in range(8):
        rows = pl.ds(part * 512, 512)
        copy = pltpu.make_async_copy(state_hbm.at[:, rows], st.at[:, rows], state_sem.at[part])
        copy.start()
        loads.append(copy)
    stiff_copy.wait()
    flipped = xs[...].T.astype(BF16)
    row_i, col_i = iota((256, 256), 0), iota((256, 256), 1)
    same_m = (row_i & 15) == (col_i & 15)
    diagonal = (row_i & 15) == (col_i >> 4)
    for n in range(16):
        pick = jnp.where(same_m & ((row_i >> 4) == n), 1.0, 0.0).astype(BF16)
        block = jnp.where(diagonal, dot(flipped, pick), 0.0)
        for u in range(2):
            w[u, pl.ds(n, 256, stride=16), :] = block[:, u * 128 : (u + 1) * 128]

    def step(g, carry):
        rows = pl.ds(pl.multiple_of(g * 256, 256), 256)
        state = jnp.concatenate([st[f, rows, :] for f in range(4)], axis=1)
        oper = jnp.concatenate([w[0, rows, :], w[1, rows, :]], axis=1).astype(BF16)
        state = state + dot(oper, state.astype(BF16))
        for e in range(16):
            cell = cell_ref[g * 16 + e]
            tile = ((cell >> 7) & 15) * 16 + (cell & 15)
            target = pl.ds(pl.multiple_of(tile * 16, 16), 16)
            for f in range(4):
                out_ref[f, target, :] = state[e * 16 : e * 16 + 16, f * 128 : f * 128 + 128]
        return carry

    for part in range(8):
        loads[part].wait()
        lax.fori_loop(part * 2, part * 2 + 2, step, 0)


def exchange_kernel(
    st, cell_ref, gcol_ref, inv, coltab_ref,
    dyn, gridb,
    halo, wv, wq, mid, req, qrow, crow,
    sel, sel_t, place, place_t,
    dyn_high, dyn_low, cols, outb, incb, backb, rcvb, flat, tend, grid,
    sx, sy, sc, rx, ry, rc,
    tx, ty, tc, ux, uy, uc,
    wsend, wrecv, vsend, vrecv, loc_sem,
    fsend, frecv, bsend, brecv, hsend, hrecv, gsend, grecv,
):
    gx, gy = lax.axis_index("gx"), lax.axis_index("gy")
    peers = Peers(gx, gy)
    barrier = pltpu.get_barrier_semaphore()

    def other_x(k):
        return lax.rem(gx + k, NX)

    def other_y(k):
        return lax.rem(gy + k, NY)

    for dgx, dgy, _, _, _, _ in CORNERS:
        pl.semaphore_signal(
            barrier, inc=1, device_id=(other_x(NX + dgx), other_y(NY + dgy)), device_id_type=MESH
        )

    def greet_x(k, carry):
        pl.semaphore_signal(barrier, inc=1, device_id=(other_x(k), gy), device_id_type=MESH)
        return carry

    def greet_y(k, carry):
        pl.semaphore_signal(barrier, inc=1, device_id=(gx, other_y(k)), device_id_type=MESH)
        return carry

    lax.fori_loop(1, NX, greet_x, 0)
    lax.fori_loop(1, NY, greet_y, 0)


    lane = iota((128, 128), 1)
    sub = iota((128, 128), 0)
    eye = lane == sub

    def to_col(row):
        return jnp.sum(jnp.where(eye, jnp.broadcast_to(row, (128, 128)), 0.0), axis=1, keepdims=True)

    def to_row(col):
        return jnp.sum(jnp.where(eye, jnp.broadcast_to(col, (128, 128)), 0.0), axis=0, keepdims=True)

    upper = jnp.where(sub < lane, 1.0, 0.0).astype(BF16)
    seen = jnp.zeros((128, 1), F32)
    want_high = jnp.zeros((128, 128), F32)
    want_low = jnp.zeros((128, 128), F32)
    for block in range(8):
        named = gcol_ref[block : block + 1, :]
        source, local = named >> 10, named & 1023
        hit = jnp.broadcast_to(source, (128, 128)) == sub
        onehot = jnp.where(hit, 1.0, 0.0)
        before = dot(onehot.astype(BF16), upper) + seen
        seen = seen + jnp.sum(onehot, axis=1, keepdims=True)
        rank = jnp.sum(jnp.where(hit, before, 0.0), axis=0, keepdims=True)
        qrow[block : block + 1, :] = peers.position(source).astype(F32) * 8.0 + rank
        ranked = jnp.broadcast_to(rank, (128, 128)) == sub.astype(F32)
        high = (local >> 5).astype(F32)
        low = (local & 31).astype(F32)
        zero = jnp.zeros((128, 128), F32)
        chosen_high = jnp.where(ranked, jnp.broadcast_to(high, (128, 128)), zero).astype(BF16)
        chosen_low = jnp.where(ranked, jnp.broadcast_to(low, (128, 128)), zero).astype(BF16)
        onehot = onehot.astype(BF16)
        want_high = want_high + dot_nt(onehot, chosen_high)
        want_low = want_low + dot_nt(onehot, chosen_low)
    wv[...] = want_high * 32.0 + want_low

    def row_out(s, carry):
        for y in range(NY):
            wq[s, y] = wv[pl.ds(s * NY + y, 1), :]
        return carry

    lax.fori_loop(0, NX, row_out, 0)
    pl.semaphore_wait(barrier, NX + NY - 2 + len(CORNERS))

    def ask_x(k, carry):
        pltpu.make_async_remote_copy(
            wq.at[other_x(k)], mid.at[gx], wsend, wrecv,
            device_id=(other_x(k), gy), device_id_type=MESH,
        ).start()
        return carry

    lax.fori_loop(1, NX, ask_x, 0)
    own_x = pltpu.make_async_copy(wq.at[gx], mid.at[gx], loc_sem.at[0])
    own_x.start()

    others_x = mid.at[pl.ds(0, NX - 1)]
    others_y = req.at[:, pl.ds(0, NY - 1)]

    def ask_y(k, carry):
        pltpu.make_async_remote_copy(
            mid.at[:, other_y(k)], req.at[:, gy], vsend, vrecv,
            device_id=(gx, other_y(k)), device_id_type=MESH,
        ).start()
        return carry

    def copy_to(src, dst, send, recv, dgx, dgy):
        return pltpu.make_async_remote_copy(
            src, dst, send, recv,
            device_id=((gx + dgx + NX) % NX, (gy + dgy + NY) % NY),
            device_id_type=MESH,
        )

    def send_halo(h):
        for f in range(2):
            field = 2 * h + f

            for k in range(16):
                part = pl.ds(k * 4, 4)
                sx[h, 0, f, part, :] = st[field, pl.ds((15 * 16 + k) * 16 + 12, 4), :]
                sx[h, 1, f, part, :] = st[field, pl.ds(k * 16, 4), :]
                sy[h, 0, f, part, :] = st[field, pl.ds((k * 16 + 15) * 16 + 3, 4, stride=4), :]
                sy[h, 1, f, part, :] = st[field, pl.ds(k * 256, 4, stride=4), :]
            for at, (_, _, _, x, y, n) in enumerate(CORNERS):
                sc[h, at, f : f + 1, :] = st[field, pl.ds((x * 16 + y) * 16 + n, 1), :]
        copies = [
            copy_to(sx.at[h, 0], rx.at[h, 0], hsend.at[h, 0], hrecv.at[h, 0], 1, 0),
            copy_to(sx.at[h, 1], rx.at[h, 1], hsend.at[h, 1], hrecv.at[h, 1], -1, 0),
            copy_to(sy.at[h, 0], ry.at[h, 0], hsend.at[h, 2], hrecv.at[h, 2], 0, 1),
            copy_to(sy.at[h, 1], ry.at[h, 1], hsend.at[h, 3], hrecv.at[h, 3], 0, -1),
        ]
        for at, (dgx, dgy, to, _, _, _) in enumerate(CORNERS):
            copies.append(
                copy_to(sc.at[h, at], rc.at[h, at], hsend.at[h, to], hrecv.at[h, to], dgx, dgy)
            )
        for copy in copies:
            copy.start()
        return copies

    def take_halo(h, copies):
        for copy in copies:
            copy.wait_recv()
        for f in range(2):
            field = 2 * h + f
            for k in range(16):
                part = pl.ds(k * 4, 4)
                halo[field, pl.ds((WEST + 1 + k) * 16 + 12, 4), :] = rx[h, 0, f, part, :]
                halo[field, pl.ds((EAST + 1 + k) * 16, 4), :] = rx[h, 1, f, part, :]
                halo[field, pl.ds((SOUTH + k) * 16 + 3, 4, stride=4), :] = ry[h, 0, f, part, :]
                halo[field, pl.ds((NORTH + k) * 16, 4, stride=4), :] = ry[h, 1, f, part, :]
            halo[field, pl.ds(WEST * 16 + 15, 1), :] = rc[h, 0, f : f + 1, :]
            halo[field, pl.ds(EAST * 16 + 3, 1), :] = rc[h, 1, f : f + 1, :]
            halo[field, pl.ds((WEST + 17) * 16 + 12, 1), :] = rc[h, 2, f : f + 1, :]
            halo[field, pl.ds((EAST + 17) * 16, 1), :] = rc[h, 3, f : f + 1, :]

    s8 = iota((8, 128), 0)
    b_at = s8 & 3
    is_b0, is_b3, first_a = b_at == 0, b_at == 3, s8 < 4
    b_scale = jnp.where(is_b0 | is_b3, 0.5, 1.0)
    scale0 = b_scale * jnp.where(first_a, 0.5, 1.0)
    scale1 = b_scale * jnp.where(first_a, 1.0, 0.5)

    def dynamics(h):
        def column(x, carry):
            fixed = isinstance(x, int)

            def rows(x, y, v):
                inside = 0 <= y < TY
                if fixed and x == -1:
                    return halo, (WEST + y + 1) * 16 + v * 8
                if fixed and x == TX:
                    return halo, (EAST + y + 1) * 16 + v * 8
                if not inside:
                    return halo, ((SOUTH if y < 0 else NORTH) + x) * 16 + v * 8
                return st, x * 256 + y * 16 + v * 8

            def load(field, x, y, v):
                ref, at = rows(x, y, v)
                return ref[field, pl.ds(at if fixed else pl.multiple_of(at, 8), 8), :]

            def along_x(y):
                found = []
                for f in range(2):
                    field = 2 * h + f
                    own0, own1 = load(field, x, y, 0), load(field, x, y, 1)
                    before, after = load(field, x - 1, y, 1), load(field, x + 1, y, 0)
                    found.append(own0 + jnp.where(first_a, pltpu.roll(before, 4, 0), 0.0))
                    found.append(own1 + jnp.where(first_a, 0.0, pltpu.roll(after, 4, 0)))
                return found

            south, here = along_x(-1), along_x(0)
            for y in range(TY):
                north = along_x(y + 1)
                for f in range(2):
                    parts = []
                    for v, scale in ((2 * f, scale0), (2 * f + 1, scale1)):
                        edge = jnp.where(is_b0, pltpu.roll(south[v], 5, 0), 0.0)
                        edge = jnp.where(is_b3, pltpu.roll(north[v], 3, 0), edge)
                        parts.append((here[v] + edge) * scale)
                    total = jnp.concatenate(parts, axis=0)
                    at = x * 256 + y * 16
                    dyn[2 * h + f, pl.ds(at if fixed else pl.multiple_of(at, 16), 16), :] = total
                    high = total.astype(BF16)
                    dyn_high[y * 16 : y * 16 + 16, f * 128 : f * 128 + 128] = high
                    low = (total - high.astype(F32)).astype(BF16)
                    dyn_low[y * 16 : y * 16 + 16, f * 128 : f * 128 + 128] = low
                south, here = here, north
            main = dot(coltab_ref[...], dyn_high[...])
            rest = dot(coltab_ref[0:64, :], dyn_low[...])
            total = main[0:64] + main[64:128] + rest
            cols[pl.ds(x * 64 if fixed else pl.multiple_of(x * 64, 64), 64), :] = total.astype(BF16)
            return carry

        column(0, 0)
        lax.fori_loop(1, TX - 1, column, 0)
        column(TX - 1, 0)

    wide = iota((128, 1024), 1)

    def selections():
        k_mask = iota((128, 128), 1) == (iota((128, 128), 0) & 7)

        def build(b, carry):
            found = peers.block(b, with_self=True)
            for part in range(2):
                asked = [
                    jnp.broadcast_to(req[tgx, tgy], (8, 128))
                    for tgx, tgy, _, _ in found[part * 16 : part * 16 + 16]
                ]
                asked = jnp.where(k_mask, jnp.concatenate(asked, axis=0), 0.0)
                asked = jnp.sum(asked, axis=1, keepdims=True).astype(I32)
                slot_at, piece = asked >> 2, asked & 3
                tile = jnp.zeros((128, 128), F32)
                for u in range(2):
                    cell = cell_ref[u : u + 1, :]
                    names = (((cell >> 7) & 15) * 16 + (cell & 15)).astype(F32)
                    names = jnp.broadcast_to(names, (128, 128))
                    tile = tile + jnp.where(slot_at == lane + 128 * u, names, 0.0)
                tile = jnp.sum(tile, axis=1, keepdims=True).astype(I32)
                at = (tile >> 4) * 64 + (piece >> 1) * 32 + (tile & 15) * 2 + (piece & 1)
                block = b * 2 + part
                rows = pl.ds(pl.multiple_of(block * 128, 128), 128)
                sel[rows, :] = jnp.where(wide == at, 1.0, 0.0).astype(BF16)
                crow[pl.ds(block, 1), :] = to_row(at.astype(F32))
            return carry

        lax.fori_loop(0, 4, build, 0)

    def transposed(row_ref, out_ref):
        def build(block, carry):
            rows = pl.ds(pl.multiple_of(block * 128, 128), 128)
            want = (sub + block * 128).astype(F32)
            for u in range(8):
                names = jnp.broadcast_to(row_ref[u : u + 1, :], (128, 128))
                out_ref[rows, u * 128 : (u + 1) * 128] = jnp.where(names == want, 1.0, 0.0).astype(BF16)
            return carry

        lax.fori_loop(0, 8, build, 0)

    def placing():
        def build(block, carry):
            rows = pl.ds(pl.multiple_of(block * 128, 128), 128)
            at = to_col(qrow[pl.ds(block, 1), :]).astype(I32)
            place[rows, :] = jnp.where(wide == at, 1.0, 0.0).astype(BF16)
            return carry

        lax.fori_loop(0, 8, build, 0)

    def permute_and_send(matrix, source, src, dst, h, send, recv, loc):
        def step(b):
            rows = pl.ds(pl.multiple_of(b * 256, 256), 256)
            moved = dot(matrix[rows, :], source[...])
            src[h, pl.ds(b * 32, 32)] = moved.reshape(32, 8, 256).astype(BF16)
            for tgx, tgy, at, back in peers.block(b):
                pltpu.make_async_remote_copy(
                    src.at[h, at], dst.at[h, back], send.at[h], recv.at[h],
                    device_id=(tgx, tgy), device_id_type=MESH,
                ).start()

        def loop_step(b, carry):
            step(b)
            return carry

        step(0)
        own = pltpu.make_async_copy(src.at[h, 0], dst.at[h, 0], loc_sem.at[loc])
        own.start()
        lax.fori_loop(1, 4, loop_step, 0)
        return own

    def wait_all(ref, h, sem):
        block = ref.at[h, pl.ds(0, ND - 1)]
        pltpu.make_async_copy(block, block, sem.at[h]).wait()

    def flatten(src, h):
        def step(block, carry):
            part = src[h, pl.ds(block * 16, 16)].astype(F32).reshape(128, 256)
            flat[pl.ds(pl.multiple_of(block * 128, 128), 128), :] = part.astype(BF16)
            return carry

        lax.fori_loop(0, 8, step, 0)

    halo_copies, forward, back_copies = [None] * NH, [None] * NH, [None] * NH
    halo_copies[0] = send_halo(0)
    own_x.wait()
    pltpu.make_async_copy(others_x, others_x, wrecv).wait()
    lax.fori_loop(1, NY, ask_y, 0)
    own_y = pltpu.make_async_copy(mid.at[:, gy], req.at[:, gy], loc_sem.at[0])
    own_y.start()
    halo_copies[1] = send_halo(1)
    for h in range(NH):
        take_halo(h, halo_copies[h])
        dynamics(h)
        if h == 0:
            own_y.wait()
            pltpu.make_async_copy(others_y, others_y, vrecv).wait()
            selections()
        forward[h] = permute_and_send(sel, cols, outb, incb, h, fsend, frecv, 1 + h)
        if h == 0:
            transposed(qrow, place_t)
            placing()

    transposed(crow, sel_t)

    def physics(h):
        def step(block, carry):
            rows = pl.ds(pl.multiple_of(block * 256, 256), 256)
            moved = dot(place[rows, :], flat[...])
            for g in range(16):
                part = moved[g * 16 : (g + 1) * 16, :]
                stacked = jnp.concatenate([part[:, :128], part[:, 128:]], axis=0)
                smooth = dot_nt(stacked.astype(BF16), inv[block * 16 + g])
                change = smooth - stacked
                change = jnp.concatenate([change[:16], change[16:]], axis=1)
                tend[pl.ds(pl.multiple_of(block * 256 + g * 16, 16), 16), :] = change.astype(BF16)
            return carry

        lax.fori_loop(0, 4, step, 0)

    for h in range(NH):
        forward[h].wait()
        wait_all(incb, h, frecv)
        flatten(incb, h)
        physics(h)
        back_copies[h] = permute_and_send(place_t, tend, backb, rcvb, h, bsend, brecv, 3 + h)

    grid[...] = jnp.zeros_like(grid)
    ring_copies = []
    for h in range(NH):
        back_copies[h].wait()
        wait_all(rcvb, h, brecv)
        flatten(rcvb, h)

        def ungroup(block, carry):
            rows = pl.ds(pl.multiple_of(block * 256, 256), 256)
            moved = dot(sel_t[rows, :], flat[...])
            for x in range(4):
                for i in range(2):
                    base = pl.multiple_of((block * 4 + x + 1) * RX + i * 40, 8)
                    piece = moved[x * 64 + i * 32 : x * 64 + i * 32 + 32, :]
                    for u in range(2):
                        grid[h, u, pl.ds(base, 32), :] = piece[:, u * 128 : (u + 1) * 128]
            return carry

        lax.fori_loop(0, 4, ungroup, 0)
        for u in range(2):
            for i in range(2):
                tx[h, 0, u, i * 32 : i * 32 + 32, :] = grid[h, u, 16 * RX + i * 40 : 16 * RX + i * 40 + 32, :]
                tx[h, 1, u, i * 32 : i * 32 + 32, :] = grid[h, u, RX + i * 40 : RX + i * 40 + 32, :]
            for j in range(2):
                ty[h, 0, u, j * 32 : j * 32 + 32, :] = grid[h, u, pl.ds(RX + 30 + j, 32, stride=40), :]
                ty[h, 1, u, j * 32 : j * 32 + 32, :] = grid[h, u, pl.ds(RX + j, 32, stride=40), :]
            for at, (_, _, _, x, y, _) in enumerate(CORNERS):
                for i in range(2):
                    base = (x + 1) * RX + i * 40 + 2 * y
                    tc[h, at, u * 4 + i * 2 : u * 4 + i * 2 + 2, :] = grid[h, u, base : base + 2, :]
        copies = [
            copy_to(tx.at[h, 0], ux.at[h, 0], gsend.at[h, 0], grecv.at[h, 0], 1, 0),
            copy_to(tx.at[h, 1], ux.at[h, 1], gsend.at[h, 1], grecv.at[h, 1], -1, 0),
            copy_to(ty.at[h, 0], uy.at[h, 0], gsend.at[h, 2], grecv.at[h, 2], 0, 1),
            copy_to(ty.at[h, 1], uy.at[h, 1], gsend.at[h, 3], grecv.at[h, 3], 0, -1),
        ]
        for at, (dgx, dgy, to, _, _, _) in enumerate(CORNERS):
            copies.append(
                copy_to(tc.at[h, at], uc.at[h, at], gsend.at[h, to], grecv.at[h, to], dgx, dgy)
            )
        for copy in copies:
            copy.start()
        ring_copies.append(copies)

    for h in range(NH):
        for copy in ring_copies[h]:
            copy.wait_recv()
        for u in range(2):
            for i in range(2):
                part = slice(i * 32, i * 32 + 32)
                grid[h, u, i * 40 : i * 40 + 32, :] = ux[h, 0, u, part, :]
                grid[h, u, 17 * RX + i * 40 : 17 * RX + i * 40 + 32, :] = ux[h, 1, u, part, :]
            for j in range(2):
                part = slice(j * 32, j * 32 + 32)
                grid[h, u, pl.ds(RX + 32 + j, 32, stride=40), :] = uy[h, 0, u, part, :]
                grid[h, u, pl.ds(RX + 34 + j, 32, stride=40), :] = uy[h, 1, u, part, :]
            for at, (big_x, base) in enumerate(((0, 32), (17, 32), (0, 34), (17, 34))):
                for i in range(2):
                    to = big_x * RX + i * 40 + base
                    grid[h, u, to : to + 2, :] = uc[h, at, u * 4 + i * 2 : u * 4 + i * 2 + 2, :]
            gridb[h, :, u * 128 : (u + 1) * 128] = grid[h, u].astype(BF16)

    pltpu.make_async_copy(others_x, others_x, wsend).wait()
    pltpu.make_async_copy(others_y, others_y, vsend).wait()
    for h in range(NH):
        wait_all(outb, h, fsend)
        wait_all(backb, h, bsend)
        for copy in halo_copies[h] + ring_copies[h]:
            copy.wait_send()


def finish_kernel(cell_ref, ret, table_ref, dyn, out_hbm, total, outv, out_sem):
    def add(x, carry):
        rows = pl.ds(pl.multiple_of(x * 256, 256), 256)
        for h in range(NH):
            near = ret[h, pl.ds(pl.multiple_of(x * RX, 16), 256), :]
            update = dot(table_ref[...], near)
            update = update[:256] + update[256:]
            for f in range(2):
                field = 2 * h + f
                total[field, rows, :] = dyn[field, rows, :] + update[:, f * 128 : (f + 1) * 128]
        return carry

    lax.fori_loop(0, TX, add, 0)

    def gather(s, carry):
        cell = cell_ref[s]
        tile = ((cell >> 7) & 15) * 16 + (cell & 15)
        source = pl.ds(pl.multiple_of(tile * 16, 16), 16)
        target = pl.ds(pl.multiple_of(s * 16, 16), 16)
        for field in range(4):
            outv[field, target, :] = total[field, source, :]
        return carry

    stores = []
    for part in range(8):
        lax.fori_loop(part * 32, part * 32 + 32, gather, 0, unroll=4)
        rows = pl.ds(part * 512, 512)
        copy = pltpu.make_async_copy(outv.at[:, rows], out_hbm.at[:, rows], out_sem.at[part])
        copy.start()
        stores.append(copy)
    for copy in stores:
        copy.wait()


def any_spec():
    return pl.BlockSpec(memory_space=pl.ANY)


def hbm_spec():
    return pl.BlockSpec(memory_space=pltpu.HBM)


def vmem_spec():
    return pl.BlockSpec(memory_space=pltpu.VMEM)


def smem_spec():
    return pl.BlockSpec(memory_space=pltpu.SMEM)


def per_device(coltab, uptab, state_in, stiffness, elem_cell, group_column, group_inverse):
    state = state_in.reshape(4, NE * 16, LEV)
    dma = pltpu.SemaphoreType.DMA
    vmem = pltpu.VMEM
    whole = jax.ShapeDtypeStruct((4, NE * 16, LEV), F32)
    combined = pl.pallas_call(
        combine_kernel,
        out_shape=whole,
        in_specs=[smem_spec(), hbm_spec(), hbm_spec()],
        out_specs=vmem_spec(),
        scratch_shapes=[
            vmem((4, NE * 16, LEV), F32),
            vmem((256, 256), F32),
            vmem((2, NE * 16, LEV), F32),
            dma,
            dma((8,)),
        ],
        compiler_params=pltpu.CompilerParams(vmem_limit_bytes=42 << 20),
        name="combine",
    )(elem_cell, state, stiffness.reshape(256, NE))
    scratch = [
        vmem((4, NHALO * 16, LEV), F32),
        vmem((128, 128), F32),
        vmem((NX, NY, 1, 128), F32),
        vmem((NX, NY, 1, 128), F32),
        vmem((NX, NY, 1, 128), F32),
        vmem((8, 128), F32),
        vmem((8, 128), F32),
        vmem((NC, NC), BF16),
        vmem((NC, NC), BF16),
        vmem((NC, NC), BF16),
        vmem((NC, NC), BF16),
        vmem((256, 256), BF16),
        vmem((256, 256), BF16),
        vmem((NC, 256), BF16),
        vmem((NH, ND, 8, 256), BF16),
        vmem((NH, ND, 8, 256), BF16),
        vmem((NH, ND, 8, 256), BF16),
        vmem((NH, ND, 8, 256), BF16),
        vmem((NC, 256), BF16),
        vmem((NC, 256), BF16),
        vmem((NH, 2, RROWS, LEV), F32),
        vmem((NH, 2, 2, 64, LEV), F32),
        vmem((NH, 2, 2, 64, LEV), F32),
        vmem((NH, 4, 8, LEV), F32),
        vmem((NH, 2, 2, 64, LEV), F32),
        vmem((NH, 2, 2, 64, LEV), F32),
        vmem((NH, 4, 8, LEV), F32),
        vmem((NH, 2, 2, 64, LEV), F32),
        vmem((NH, 2, 2, 64, LEV), F32),
        vmem((NH, 4, 8, LEV), F32),
        vmem((NH, 2, 2, 64, LEV), F32),
        vmem((NH, 2, 2, 64, LEV), F32),
        vmem((NH, 4, 8, LEV), F32),
        dma, dma, dma, dma, dma((5,)),
        dma((NH,)), dma((NH,)), dma((NH,)), dma((NH,)),
        dma((NH, 8)), dma((NH, 8)), dma((NH, 8)), dma((NH, 8)),
    ]
    dyn, ret = pl.pallas_call(
        exchange_kernel,
        out_shape=(whole, jax.ShapeDtypeStruct((NH, RROWS, 256), BF16)),
        in_specs=[vmem_spec()] * 5,
        out_specs=(vmem_spec(), vmem_spec()),
        scratch_shapes=scratch,
        compiler_params=pltpu.CompilerParams(
            collective_id=0, has_side_effects=True, vmem_limit_bytes=28 << 20
        ),
        name="exchange",
    )(combined, elem_cell.reshape(2, 128), group_column.reshape(8, 128), group_inverse, coltab)
    out = pl.pallas_call(
        finish_kernel,
        out_shape=whole,
        in_specs=[smem_spec(), vmem_spec(), vmem_spec(), vmem_spec()],
        out_specs=any_spec(),
        scratch_shapes=[vmem((4, NE * 16, LEV), F32), vmem((4, NE * 16, LEV), F32), dma((8,))],
        compiler_params=pltpu.CompilerParams(vmem_limit_bytes=32 << 20),
        name="finish",
    )(elem_cell, ret, uptab, dyn)
    return out.reshape(4, NE, 16, LEV)


def solution(mesh):
    coltab, uptab = constant_tables()
    placed = (
        P(None, ("gx", "gy"), None, None),
        P(None, None, ("gx", "gy")),
        P(("gx", "gy")),
        P(("gx", "gy")),
        P(("gx", "gy"), None, None),
    )

    def run(*args):
        body = functools.partial(per_device, jnp.asarray(coltab), jnp.asarray(uptab))
        return jax.shard_map(
            body,
            mesh=mesh,
            in_specs=placed,
            out_specs=P(None, ("gx", "gy"), None, None),
            check_vma=False,
        )(*args)

    return run
```

time: 418 us -> 78.6 us (0.19)
  local copies, waits for them, and re-layouts: 195 us -> 1.65 us
  other arithmetic: 87.3 us -> 0 us
  Pallas kernels: 0 us -> 76.7 us
  matrix products: 68.4 us -> 0 us
  starting transfers between devices: 38.1 us -> 0 us
  waiting for transfers between devices: 25.5 us -> 0 us
    gather x10 -> x0, local copies, waits for them, and re-layouts: 105 us -> none  [the longest x1 33.6 us: per_device(): jnp.take(combined, node_order, axis=1)]
    pallas_call x0 -> x3, Pallas kernels: none -> 76.7 us  [the longest x1 61.7 us: per_device(): pl.pallas_call(exchange_kernel, out_shape=(whole, jax.ShapeDtypeStruct((N...]
    dot_general x6 -> x0, matrix products: 68.4 us -> none  [the longest x2 30.6 us: per_device(): jnp.einsum('ia,jb,fxaybl->fxyijl', halves, halves, split_nodes, precision...]
    select_n x10 -> x0, other arithmetic: 34.9 us -> none  [the longest x1 16.8 us: per_device(): jnp.take(combined, node_order, axis=1)]
    add x5 -> x0, other arithmetic: 30.2 us -> none  [the longest x2 15.7 us: add_shared(): middle + jnp.where(position == 0, preceding, 0.0)]
    scatter x4 -> x0, local copies, waits for them, and re-layouts: 26 us -> none  [the longest x1 15.5 us: per_device(): slot_order = jnp.zeros((elements * 16,), jnp.int32).at[node_order].set(jn...]
    reshape x5 -> x0, local copies, waits for them, and re-layouts: 25.5 us -> none  [the longest x1 18.6 us: per_device(): combined = (state_in + local_term).reshape(fields, elements * 16, levels)]
    all_to_all x3 -> x0, starting transfers between devices: 22.3 us -> none  [the longest x1 11.5 us: per_device(): lax.all_to_all(wanted, ('gx', 'gy'), split_axis=0, concat_axis=0, tiled=T...]
  transfers between devices with their start and end apart: 11 -> 0, of which waited for: 6 -> 0; matrix products, arithmetic and copies ran while one was open for 32% -> 0% of each run, Pallas kernels for 0% -> 0%
where the time goes in v1:
time: 78.6 us; the launch traced here: 78.4 us
  Pallas kernels  76.7 us (98%)
  local copies, waits for them, and re-layouts  1.65 us (2%)
    pallas_call x1, Pallas kernels, per_device(): pl.pallas_call(exchange_kernel, out_shape=(whole, jax.ShapeDtypeStruct((N...  61.7 us
    pallas_call x1, Pallas kernels, per_device(): pl.pallas_call(finish_kernel, out_shape=whole, in_specs=[smem_spec(), vme...  8.85 us
    pallas_call x1, Pallas kernels, per_device(): pl.pallas_call(combine_kernel, out_shape=whole, in_specs=[smem_spec(), hb...  6.13 us
    unnamed x12, local copies, waits for them, and re-layouts  1.65 us

profile of v1, /device:TPU:1, one launch (start us, length us, event | category | flops | bytes accessed | tf_op | source)
XLA Modules:
  0.0 78.4 jit_solution(14793521815759300085)
XLA Ops:
  0.0 0.0 copy-start.1
  0.0 0.9 %copy-done.1 = f32[16,16,256]{2,1,0:T(8,128)S(1)} copy-done((f32[16,16,256]{2,1,0:T(8,128)S(1)}, f32[16,16,256]{2,1,0:T(8,128)}, u32[]{:S(2)}) %copy-start.1) | copy-done | bytes 262168
  1.0 0.0 copy-start.4
  1.0 0.7 copy-done.4
  1.6 0.0 copy-start
  1.6 0.0 copy-start.3
  1.6 0.0 copy-start.5
  1.6 6.1 %combine.1.st = f32[4,4096,128]{2,1,0:T(8,128)S(1)} custom-call(s32[256]{0:T(256)S(1)} %copy-done.4, f32[4,4096,128]{2,1,0:T(8,128)} %bitcast.8, f32[256,256]{1,0:T(8,128)S(1)} %bitcast.5), custom_call_target="tpu_custom_call" | custom-call | tf_op jit(solution)/shard_map/combine/pallas_call | solution.py:636
  7.8 0.0 copy-done
  7.8 0.0 copy-done.3
  7.8 0.0 copy-done.5
  7.8 0.0 copy-start.2
  7.8 61.7 %exchange.1 = (f32[4,4096,128]{2,1,0:T(8,128)S(1)}, bf16[2,1456,256]{2,1,0:T(8,128)(2,1)S(1)}) custom-call(f32[4,4096,128]{2,1,0:T(8,128)S(1)} %combine.1.st, s32[2,128]{1,0:T(2,128)S(1)} %bitcast.6, s32[8,128]{1,0:T(8,128)S(1)} %bitcast.7, bf16[64,128,128]{2,1,0:T(8,128)(2,1)S(1)} %copy-done, bf16[128,256]{1,0:T(8,128)(2,1)S(1)} %copy-done.3), custom_call_target="tpu_custom_call" | custom-call | tf_op jit(solution)/shard_map/exchange/pallas_call | solution.py:689
  69.6 0.0 copy-done.2
  69.6 8.9 %finish.1 = f32[4,4096,128]{2,1,0:T(8,128)} custom-call(s32[256]{0:T(256)S(1)} %copy-done.4, bf16[2,1456,256]{2,1,0:T(8,128)(2,1)S(1)} %get-tuple-element.7.ret, bf16[512,256]{1,0:T(8,128)(2,1)S(1)} %copy-done.2, f32[4,4096,128]{2,1,0:T(8,128)S(1)} %get-tuple-element.8.dyn), custom_call_target="tpu_custom_call" | custom-call | tf_op jit(solution)/shard_map/finish/pallas_call | solution.py:700
Async XLA Ops:
  0.0 0.9 %copy-start.1 = (f32[16,16,256]{2,1,0:T(8,128)S(1)}, f32[16,16,256]{2,1,0:T(8,128)}, u32[]{:S(2)}) copy-start(f32[16,16,256]{2,1,0:T(8,128)} %param.8) | copy-start | bytes 786436
  1.0 0.7 copy-start.4
  1.6 6.1 %copy-start = (bf16[64,128,128]{2,1,0:T(8,128)(2,1)S(1)}, bf16[64,128,128]{2,1,0:T(8,128)(2,1)}, u32[]{:S(2)}) copy-start(bf16[64,128,128]{2,1,0:T(8,128)(2,1)} %inv.1) | copy-start | bytes 6291460
  1.6 6.2 %copy-start.3 = (bf16[128,256]{1,0:T(8,128)(2,1)S(1)}, bf16[128,256]{1,0:T(8,128)(2,1)}, u32[]{:S(2)}) copy-start(bf16[128,256]{1,0:T(8,128)(2,1)} %constant.4.clone.coltab_ref) | copy-start | bytes 196612
  1.6 6.2 %copy-start.5 = (s32[1024]{0:T(1024)S(1)}, s32[1024]{0:T(1024)}, u32[]{:S(2)}) copy-start(s32[1024]{0:T(1024)} %param.10) | copy-start | bytes 12292
  7.8 61.8 %copy-start.2 = (bf16[512,256]{1,0:T(8,128)(2,1)S(1)}, bf16[512,256]{1,0:T(8,128)(2,1)}, u32[]{:S(2)}) copy-start(bf16[512,256]{1,0:T(8,128)(2,1)} %constant.5.clone.table_ref) | copy-start | bytes 786436

commit v2 on v1

--- a/solution.py
+++ b/solution.py
@@ -129,55 +129,19 @@
         return b * 32 + d * 8 + a * 2 + c
 
 
-def combine_kernel(cell_ref, state_hbm, stiff_hbm, out_ref, st, xs, w, stiff_sem, state_sem):
-    stiff_copy = pltpu.make_async_copy(stiff_hbm, xs, stiff_sem)
-    stiff_copy.start()
-    loads = []
-    for part in range(8):
-        rows = pl.ds(part * 512, 512)
-        copy = pltpu.make_async_copy(state_hbm.at[:, rows], st.at[:, rows], state_sem.at[part])
-        copy.start()
-        loads.append(copy)
-    stiff_copy.wait()
-    flipped = xs[...].T.astype(BF16)
-    row_i, col_i = iota((256, 256), 0), iota((256, 256), 1)
-    same_m = (row_i & 15) == (col_i & 15)
-    diagonal = (row_i & 15) == (col_i >> 4)
-    for n in range(16):
-        pick = jnp.where(same_m & ((row_i >> 4) == n), 1.0, 0.0).astype(BF16)
-        block = jnp.where(diagonal, dot(flipped, pick), 0.0)
-        for u in range(2):
-            w[u, pl.ds(n, 256, stride=16), :] = block[:, u * 128 : (u + 1) * 128]
-
-    def step(g, carry):
-        rows = pl.ds(pl.multiple_of(g * 256, 256), 256)
-        state = jnp.concatenate([st[f, rows, :] for f in range(4)], axis=1)
-        oper = jnp.concatenate([w[0, rows, :], w[1, rows, :]], axis=1).astype(BF16)
-        state = state + dot(oper, state.astype(BF16))
-        for e in range(16):
-            cell = cell_ref[g * 16 + e]
-            tile = ((cell >> 7) & 15) * 16 + (cell & 15)
-            target = pl.ds(pl.multiple_of(tile * 16, 16), 16)
-            for f in range(4):
-                out_ref[f, target, :] = state[e * 16 : e * 16 + 16, f * 128 : f * 128 + 128]
-        return carry
-
-    for part in range(8):
-        loads[part].wait()
-        lax.fori_loop(part * 2, part * 2 + 2, step, 0)
-
-
 def exchange_kernel(
-    st, cell_ref, gcol_ref, inv, coltab_ref,
-    dyn, gridb,
+    state_hbm, stiff_hbm, inv_hbm, cell_ref, gcol_ref, coltab_ref, uptab_ref,
+    dyn,
+    inv, st0, st1, xs, w16, slot_vmem, slots,
     halo, wv, wq, mid, req, qrow, crow,
     sel, sel_t, place, place_t,
-    dyn_high, dyn_low, cols, outb, incb, backb, rcvb, flat, tend, grid,
+    dyn_high, dyn_low, cols, outb, incb, backb, rcvb, flat, tend, grid, gridb,
     sx, sy, sc, rx, ry, rc,
     tx, ty, tc, ux, uy, uc,
-    wsend, wrecv, vsend, vrecv, loc_sem,
+    state_sem, in_sem, wsend, wrecv, vsend, vrecv, loc_sem,
     fsend, frecv, bsend, brecv, hsend, hrecv, gsend, grecv,
 ):
+    st = (st0, st1)
     gx, gy = lax.axis_index("gx"), lax.axis_index("gy")
     peers = Peers(gx, gy)
     barrier = pltpu.get_barrier_semaphore()
@@ -205,6 +169,23 @@
     lax.fori_loop(1, NY, greet_y, 0)
 
 
+    stiff_copy = pltpu.make_async_copy(stiff_hbm, xs, in_sem.at[0])
+    stiff_copy.start()
+    state_copies = []
+    for h in range(NH):
+        row = []
+        for part in range(4):
+            elems = pl.ds(part * 64, 64)
+            copy = pltpu.make_async_copy(
+                state_hbm.at[pl.ds(2 * h, 2), elems], st[h].at[:, elems], state_sem.at[h, part]
+            )
+            copy.start()
+            row.append(copy)
+        state_copies.append(row)
+
+    inv_copy = pltpu.make_async_copy(inv_hbm, inv, in_sem.at[2])
+    inv_copy.start()
+
     lane = iota((128, 128), 1)
     sub = iota((128, 128), 0)
     eye = lane == sub
@@ -214,6 +195,20 @@
 
     def to_row(col):
         return jnp.sum(jnp.where(eye, jnp.broadcast_to(col, (128, 128)), 0.0), axis=0, keepdims=True)
+
+    def tiles(u):
+        cell = cell_ref[u : u + 1, :]
+        return (((cell >> 7) & 15) * 16 + (cell & 15)).astype(F32)
+
+    for v in range(2):
+        found = jnp.zeros((128, 128), F32)
+        for u in range(2):
+            at = to_col(tiles(u))
+            number = (sub + 128 * u).astype(F32)
+            found = jnp.maximum(found, jnp.where(at == (lane + 128 * v).astype(F32), number, 0.0))
+        slot_vmem[v : v + 1, :] = jnp.max(found, axis=0, keepdims=True).astype(I32)
+    slot_copy = pltpu.make_async_copy(slot_vmem, slots, in_sem.at[1])
+    slot_copy.start()
 
     upper = jnp.where(sub < lane, 1.0, 0.0).astype(BF16)
     seen = jnp.zeros((128, 1), F32)
@@ -245,6 +240,17 @@
         return carry
 
     lax.fori_loop(0, NX, row_out, 0)
+    stiff_copy.wait()
+    flipped = xs[...].T.astype(BF16)
+    row_i, col_i = iota((256, 256), 0), iota((256, 256), 1)
+    same_m = (row_i & 15) == (col_i & 15)
+    diagonal = (row_i & 15) == (col_i >> 4)
+    for n in range(16):
+        pick = jnp.where(same_m & ((row_i >> 4) == n), 1.0, 0.0).astype(BF16)
+        block = jnp.where(diagonal, dot(flipped, pick), 0.0)
+        for u in range(2):
+            dyn[u, pl.ds(n, 256, stride=16), :] = block[:, u * 128 : (u + 1) * 128]
+
     pl.semaphore_wait(barrier, NX + NY - 2 + len(CORNERS))
 
     def ask_x(k, carry):
@@ -268,6 +274,30 @@
         ).start()
         return carry
 
+    def combine(h):
+        def step(g, carry):
+            rows = pl.ds(pl.multiple_of(g * 256, 256), 256)
+            elems = pl.ds(g * 16, 16)
+            both = jnp.concatenate([st[h][f, elems].reshape(256, LEV) for f in range(2)], axis=1)
+            if h == 0:
+                oper = jnp.concatenate([dyn[0, rows, :], dyn[1, rows, :]], axis=1).astype(BF16)
+                w16[rows, :] = oper
+            else:
+                oper = w16[rows, :]
+            both = both + dot(oper, both.astype(BF16))
+            for f in range(2):
+                st[h][f, elems] = both[:, f * LEV : (f + 1) * LEV].reshape(16, 16, LEV)
+            return carry
+
+        for part in range(4):
+            state_copies[h][part].wait()
+            lax.fori_loop(part * 4, part * 4 + 4, step, 0)
+
+    def slot(x, y):
+        if isinstance(x, int):
+            return slots[x // 8, x % 8 * 16 + y] & (NE - 1)
+        return slots[lax.div(x, 8), lax.rem(x, 8) * 16 + y] & (NE - 1)
+
     def copy_to(src, dst, send, recv, dgx, dgy):
         return pltpu.make_async_remote_copy(
             src, dst, send, recv,
@@ -281,12 +311,18 @@
 
             for k in range(16):
                 part = pl.ds(k * 4, 4)
-                sx[h, 0, f, part, :] = st[field, pl.ds((15 * 16 + k) * 16 + 12, 4), :]
-                sx[h, 1, f, part, :] = st[field, pl.ds(k * 16, 4), :]
-                sy[h, 0, f, part, :] = st[field, pl.ds((k * 16 + 15) * 16 + 3, 4, stride=4), :]
-                sy[h, 1, f, part, :] = st[field, pl.ds(k * 256, 4, stride=4), :]
+                sx[h, 0, f, part, :] = st[h][f, slot(15, k), 8:16, :][4:8]
+                sx[h, 1, f, part, :] = st[h][f, slot(0, k), 0:8, :][0:4]
+                for side, y, b in ((0, 15, 3), (1, 0, 0)):
+                    at = slot(k, y)
+                    for v in range(2):
+                        half = st[h][f, at, v * 8 : v * 8 + 8, :]
+                        for a in range(2):
+                            to = k * 4 + v * 2 + a
+                            sy[h, side, f, to : to + 1, :] = half[a * 4 + b : a * 4 + b + 1]
             for at, (_, _, _, x, y, n) in enumerate(CORNERS):
-                sc[h, at, f : f + 1, :] = st[field, pl.ds((x * 16 + y) * 16 + n, 1), :]
+                half = st[h][f, slot(x, y), n // 8 * 8 : n // 8 * 8 + 8, :]
+                sc[h, at, f : f + 1, :] = half[n % 8 : n % 8 + 1]
         copies = [
             copy_to(sx.at[h, 0], rx.at[h, 0], hsend.at[h, 0], hrecv.at[h, 0], 1, 0),
             copy_to(sx.at[h, 1], rx.at[h, 1], hsend.at[h, 1], hrecv.at[h, 1], -1, 0),
@@ -308,14 +344,14 @@
             field = 2 * h + f
             for k in range(16):
                 part = pl.ds(k * 4, 4)
-                halo[field, pl.ds((WEST + 1 + k) * 16 + 12, 4), :] = rx[h, 0, f, part, :]
-                halo[field, pl.ds((EAST + 1 + k) * 16, 4), :] = rx[h, 1, f, part, :]
-                halo[field, pl.ds((SOUTH + k) * 16 + 3, 4, stride=4), :] = ry[h, 0, f, part, :]
-                halo[field, pl.ds((NORTH + k) * 16, 4, stride=4), :] = ry[h, 1, f, part, :]
-            halo[field, pl.ds(WEST * 16 + 15, 1), :] = rc[h, 0, f : f + 1, :]
-            halo[field, pl.ds(EAST * 16 + 3, 1), :] = rc[h, 1, f : f + 1, :]
-            halo[field, pl.ds((WEST + 17) * 16 + 12, 1), :] = rc[h, 2, f : f + 1, :]
-            halo[field, pl.ds((EAST + 17) * 16, 1), :] = rc[h, 3, f : f + 1, :]
+                halo[field, WEST + 1 + k, 12:16, :] = rx[h, 0, f, part, :]
+                halo[field, EAST + 1 + k, 0:4, :] = rx[h, 1, f, part, :]
+                halo[field, SOUTH + k, pl.ds(3, 4, stride=4), :] = ry[h, 0, f, part, :]
+                halo[field, NORTH + k, pl.ds(0, 4, stride=4), :] = ry[h, 1, f, part, :]
+            halo[field, WEST, 15:16, :] = rc[h, 0, f : f + 1, :]
+            halo[field, EAST, 3:4, :] = rc[h, 1, f : f + 1, :]
+            halo[field, WEST + 17, 12:13, :] = rc[h, 2, f : f + 1, :]
+            halo[field, EAST + 17, 0:1, :] = rc[h, 3, f : f + 1, :]
 
     s8 = iota((8, 128), 0)
     b_at = s8 & 3
@@ -328,26 +364,29 @@
         def column(x, carry):
             fixed = isinstance(x, int)
 
-            def rows(x, y, v):
-                inside = 0 <= y < TY
+            def inside(x, y):
+                return 0 <= y < TY and not (fixed and not 0 <= x < TX)
+
+            def locate(x, y):
+                if inside(x, y):
+                    return slot(x, y)
                 if fixed and x == -1:
-                    return halo, (WEST + y + 1) * 16 + v * 8
+                    return WEST + y + 1
                 if fixed and x == TX:
-                    return halo, (EAST + y + 1) * 16 + v * 8
-                if not inside:
-                    return halo, ((SOUTH if y < 0 else NORTH) + x) * 16 + v * 8
-                return st, x * 256 + y * 16 + v * 8
-
-            def load(field, x, y, v):
-                ref, at = rows(x, y, v)
-                return ref[field, pl.ds(at if fixed else pl.multiple_of(at, 8), 8), :]
+                    return EAST + y + 1
+                return (SOUTH if y < 0 else NORTH) + x
+
+            def load(f, x, y, at, v):
+                if inside(x, y):
+                    return st[h][f, at, v * 8 : v * 8 + 8, :]
+                return halo[2 * h + f, at, v * 8 : v * 8 + 8, :]
 
             def along_x(y):
                 found = []
+                mine, west, east = locate(x, y), locate(x - 1, y), locate(x + 1, y)
                 for f in range(2):
-                    field = 2 * h + f
-                    own0, own1 = load(field, x, y, 0), load(field, x, y, 1)
-                    before, after = load(field, x - 1, y, 1), load(field, x + 1, y, 0)
+                    own0, own1 = load(f, x, y, mine, 0), load(f, x, y, mine, 1)
+                    before, after = load(f, x - 1, y, west, 1), load(f, x + 1, y, east, 0)
                     found.append(own0 + jnp.where(first_a, pltpu.roll(before, 4, 0), 0.0))
                     found.append(own1 + jnp.where(first_a, 0.0, pltpu.roll(after, 4, 0)))
                 return found
@@ -396,9 +435,7 @@
                 slot_at, piece = asked >> 2, asked & 3
                 tile = jnp.zeros((128, 128), F32)
                 for u in range(2):
-                    cell = cell_ref[u : u + 1, :]
-                    names = (((cell >> 7) & 15) * 16 + (cell & 15)).astype(F32)
-                    names = jnp.broadcast_to(names, (128, 128))
+                    names = jnp.broadcast_to(tiles(u), (128, 128))
                     tile = tile + jnp.where(slot_at == lane + 128 * u, names, 0.0)
                 tile = jnp.sum(tile, axis=1, keepdims=True).astype(I32)
                 at = (tile >> 4) * 64 + (piece >> 1) * 32 + (tile & 15) * 2 + (piece & 1)
@@ -464,13 +501,19 @@
         lax.fori_loop(0, 8, step, 0)
 
     halo_copies, forward, back_copies = [None] * NH, [None] * NH, [None] * NH
-    halo_copies[0] = send_halo(0)
+    combine(0)
     own_x.wait()
     pltpu.make_async_copy(others_x, others_x, wrecv).wait()
     lax.fori_loop(1, NY, ask_y, 0)
     own_y = pltpu.make_async_copy(mid.at[:, gy], req.at[:, gy], loc_sem.at[0])
     own_y.start()
+    slot_copy.wait()
+    halo_copies[0] = send_halo(0)
+    combine(1)
     halo_copies[1] = send_halo(1)
+    transposed(qrow, place_t)
+    placing()
+    grid[...] = jnp.zeros_like(grid)
     for h in range(NH):
         take_halo(h, halo_copies[h])
         dynamics(h)
@@ -479,11 +522,9 @@
             pltpu.make_async_copy(others_y, others_y, vrecv).wait()
             selections()
         forward[h] = permute_and_send(sel, cols, outb, incb, h, fsend, frecv, 1 + h)
-        if h == 0:
-            transposed(qrow, place_t)
-            placing()
 
     transposed(crow, sel_t)
+    inv_copy.wait()
 
     def physics(h):
         def step(block, carry):
@@ -507,8 +548,21 @@
         physics(h)
         back_copies[h] = permute_and_send(place_t, tend, backb, rcvb, h, bsend, brecv, 3 + h)
 
-    grid[...] = jnp.zeros_like(grid)
     ring_copies = []
+
+    def finish(h):
+        def add(x, carry):
+            rows = pl.ds(pl.multiple_of(x * 256, 256), 256)
+            near = gridb[pl.ds(pl.multiple_of(x * RX, 16), 256), :]
+            update = dot(uptab_ref[...], near)
+            update = update[:256] + update[256:]
+            for f in range(2):
+                field = 2 * h + f
+                dyn[field, rows, :] = dyn[field, rows, :] + update[:, f * LEV : (f + 1) * LEV]
+            return carry
+
+        lax.fori_loop(0, TX, add, 0)
+
     for h in range(NH):
         back_copies[h].wait()
         wait_all(rcvb, h, brecv)
@@ -550,9 +604,7 @@
         for copy in copies:
             copy.start()
         ring_copies.append(copies)
-
-    for h in range(NH):
-        for copy in ring_copies[h]:
+        for copy in copies:
             copy.wait_recv()
         for u in range(2):
             for i in range(2):
@@ -567,7 +619,9 @@
                 for i in range(2):
                     to = big_x * RX + i * 40 + base
                     grid[h, u, to : to + 2, :] = uc[h, at, u * 4 + i * 2 : u * 4 + i * 2 + 2, :]
-            gridb[h, :, u * 128 : (u + 1) * 128] = grid[h, u].astype(BF16)
+            gridb[:, u * 128 : (u + 1) * 128] = grid[h, u].astype(BF16)
+        finish(h)
+
 
     pltpu.make_async_copy(others_x, others_x, wsend).wait()
     pltpu.make_async_copy(others_y, others_y, vsend).wait()
@@ -578,38 +632,17 @@
             copy.wait_send()
 
 
-def finish_kernel(cell_ref, ret, table_ref, dyn, out_hbm, total, outv, out_sem):
-    def add(x, carry):
-        rows = pl.ds(pl.multiple_of(x * 256, 256), 256)
-        for h in range(NH):
-            near = ret[h, pl.ds(pl.multiple_of(x * RX, 16), 256), :]
-            update = dot(table_ref[...], near)
-            update = update[:256] + update[256:]
-            for f in range(2):
-                field = 2 * h + f
-                total[field, rows, :] = dyn[field, rows, :] + update[:, f * 128 : (f + 1) * 128]
+def place_kernel(cell_ref, total, out_hbm, sem):
+    def step(s, carry):
+        for k in range(8):
+            at = s * 8 + k
+            cell = cell_ref[at]
+            tile = ((cell >> 7) & 15) * 16 + (cell & 15)
+            pltpu.make_async_copy(total.at[:, tile], out_hbm.at[:, at], sem).start()
         return carry
 
-    lax.fori_loop(0, TX, add, 0)
-
-    def gather(s, carry):
-        cell = cell_ref[s]
-        tile = ((cell >> 7) & 15) * 16 + (cell & 15)
-        source = pl.ds(pl.multiple_of(tile * 16, 16), 16)
-        target = pl.ds(pl.multiple_of(s * 16, 16), 16)
-        for field in range(4):
-            outv[field, target, :] = total[field, source, :]
-        return carry
-
-    stores = []
-    for part in range(8):
-        lax.fori_loop(part * 32, part * 32 + 32, gather, 0, unroll=4)
-        rows = pl.ds(part * 512, 512)
-        copy = pltpu.make_async_copy(outv.at[:, rows], out_hbm.at[:, rows], out_sem.at[part])
-        copy.start()
-        stores.append(copy)
-    for copy in stores:
-        copy.wait()
+    lax.fori_loop(0, NE // 8, step, 0)
+    pltpu.make_async_copy(total, out_hbm, sem).wait()
 
 
 def any_spec():
@@ -629,27 +662,17 @@
 
 
 def per_device(coltab, uptab, state_in, stiffness, elem_cell, group_column, group_inverse):
-    state = state_in.reshape(4, NE * 16, LEV)
     dma = pltpu.SemaphoreType.DMA
     vmem = pltpu.VMEM
-    whole = jax.ShapeDtypeStruct((4, NE * 16, LEV), F32)
-    combined = pl.pallas_call(
-        combine_kernel,
-        out_shape=whole,
-        in_specs=[smem_spec(), hbm_spec(), hbm_spec()],
-        out_specs=vmem_spec(),
-        scratch_shapes=[
-            vmem((4, NE * 16, LEV), F32),
-            vmem((256, 256), F32),
-            vmem((2, NE * 16, LEV), F32),
-            dma,
-            dma((8,)),
-        ],
-        compiler_params=pltpu.CompilerParams(vmem_limit_bytes=42 << 20),
-        name="combine",
-    )(elem_cell, state, stiffness.reshape(256, NE))
     scratch = [
-        vmem((4, NHALO * 16, LEV), F32),
+        vmem((64, LEV, LEV), BF16),
+        vmem((2, NE, 16, LEV), F32),
+        vmem((2, NE, 16, LEV), F32),
+        vmem((256, 256), F32),
+        vmem((NE * 16, 256), BF16),
+        vmem((2, 128), I32),
+        pltpu.SMEM((2, 128), I32),
+        vmem((4, NHALO, 16, LEV), F32),
         vmem((128, 128), F32),
         vmem((NX, NY, 1, 128), F32),
         vmem((NX, NY, 1, 128), F32),
@@ -670,6 +693,7 @@
         vmem((NC, 256), BF16),
         vmem((NC, 256), BF16),
         vmem((NH, 2, RROWS, LEV), F32),
+        vmem((RROWS, 256), BF16),
         vmem((NH, 2, 2, 64, LEV), F32),
         vmem((NH, 2, 2, 64, LEV), F32),
         vmem((NH, 4, 8, LEV), F32),
@@ -682,31 +706,33 @@
         vmem((NH, 2, 2, 64, LEV), F32),
         vmem((NH, 2, 2, 64, LEV), F32),
         vmem((NH, 4, 8, LEV), F32),
-        dma, dma, dma, dma, dma((5,)),
+        dma((NH, 4)), dma((3,)), dma, dma, dma, dma, dma((5,)),
         dma((NH,)), dma((NH,)), dma((NH,)), dma((NH,)),
         dma((NH, 8)), dma((NH, 8)), dma((NH, 8)), dma((NH, 8)),
     ]
-    dyn, ret = pl.pallas_call(
+    total = pl.pallas_call(
         exchange_kernel,
-        out_shape=(whole, jax.ShapeDtypeStruct((NH, RROWS, 256), BF16)),
-        in_specs=[vmem_spec()] * 5,
-        out_specs=(vmem_spec(), vmem_spec()),
+        out_shape=jax.ShapeDtypeStruct((4, NE * 16, LEV), F32),
+        in_specs=[any_spec()] * 3 + [vmem_spec()] * 4,
+        out_specs=vmem_spec(),
         scratch_shapes=scratch,
         compiler_params=pltpu.CompilerParams(
-            collective_id=0, has_side_effects=True, vmem_limit_bytes=28 << 20
+            collective_id=0, has_side_effects=True, vmem_limit_bytes=43 << 20
         ),
         name="exchange",
-    )(combined, elem_cell.reshape(2, 128), group_column.reshape(8, 128), group_inverse, coltab)
-    out = pl.pallas_call(
-        finish_kernel,
-        out_shape=whole,
-        in_specs=[smem_spec(), vmem_spec(), vmem_spec(), vmem_spec()],
+    )(
+        state_in, stiffness.reshape(256, NE), group_inverse, elem_cell.reshape(2, 128),
+        group_column.reshape(8, 128), coltab, uptab,
+    )
+    return pl.pallas_call(
+        place_kernel,
+        out_shape=jax.ShapeDtypeStruct((4, NE, 16, LEV), F32),
+        in_specs=[smem_spec(), vmem_spec()],
         out_specs=any_spec(),
-        scratch_shapes=[vmem((4, NE * 16, LEV), F32), vmem((4, NE * 16, LEV), F32), dma((8,))],
-        compiler_params=pltpu.CompilerParams(vmem_limit_bytes=32 << 20),
-        name="finish",
-    )(elem_cell, ret, uptab, dyn)
-    return out.reshape(4, NE, 16, LEV)
+        scratch_shapes=[dma],
+        compiler_params=pltpu.CompilerParams(vmem_limit_bytes=4 << 20),
+        name="place",
+    )(elem_cell, total.reshape(4, NE, 16, LEV))
 
 
 def solution(mesh):

time: 78.6 us -> 83.7 us (1.065)
  local copies, waits for them, and re-layouts: 1.65 us -> 5.69 us
    unnamed x12, local copies, waits for them, and re-layouts: 1.65 us -> 5.69 us
    pallas_call x3 -> x2, Pallas kernels: 76.7 us -> 77.5 us  [the longest x1 73.7 us: per_device(): pl.pallas_call(exchange_kernel, out_shape=jax.ShapeDtypeStruct((4, NE * 1...]
where the time goes in v2:
time: 83.7 us; the launch traced here: 83.2 us
  Pallas kernels  77.5 us (93%)
  local copies, waits for them, and re-layouts  5.69 us (7%)
    pallas_call x1, Pallas kernels, per_device(): pl.pallas_call(exchange_kernel, out_shape=jax.ShapeDtypeStruct((4, NE * 1...  73.7 us
    unnamed x12, local copies, waits for them, and re-layouts  5.69 us
    pallas_call x1, Pallas kernels, per_device(): pl.pallas_call(place_kernel, out_shape=jax.ShapeDtypeStruct((4, NE, 16, L...  3.73 us

profile of v2, /device:TPU:1, one launch (start us, length us, event | category | flops | bytes accessed | tf_op | source)
XLA Modules:
  0.0 83.2 jit_solution(14106094257686420371)
XLA Ops:
  0.0 0.0 copy-start
  0.0 1.6 %copy-done = bf16[64,128,128]{2,1,0:T(8,128)(2,1)S(1)} copy-done((bf16[64,128,128]{2,1,0:T(8,128)(2,1)S(1)}, bf16[64,128,128]{2,1,0:T(8,128)(2,1)}, u32[]{:S(2)}) %copy-start) | copy-done | bytes 2097176
  1.6 0.0 copy-start.1
  1.6 0.9 %copy-done.1 = f32[16,16,256]{2,1,0:T(8,128)S(1)} copy-done((f32[16,16,256]{2,1,0:T(8,128)S(1)}, f32[16,16,256]{2,1,0:T(8,128)}, u32[]{:S(2)}) %copy-start.1) | copy-done | bytes 262168
  2.5 0.0 copy-start.2
  2.5 0.9 %copy-done.2 = bf16[512,256]{1,0:T(8,128)(2,1)S(1)} copy-done((bf16[512,256]{1,0:T(8,128)(2,1)S(1)}, bf16[512,256]{1,0:T(8,128)(2,1)}, u32[]{:S(2)}) %copy-start.2) | copy-done | bytes 262168
  3.5 0.0 copy-start.3
  3.5 0.8 %copy-done.3 = bf16[128,256]{1,0:T(8,128)(2,1)S(1)} copy-done((bf16[128,256]{1,0:T(8,128)(2,1)S(1)}, bf16[128,256]{1,0:T(8,128)(2,1)}, u32[]{:S(2)}) %copy-start.3) | copy-done | bytes 65560
  4.3 0.0 copy-start.4
  4.3 0.7 copy-done.4
  5.0 0.0 copy-start.5
  5.0 0.7 copy-done.5
  5.7 73.7 %exchange.1 = f32[4,4096,128]{2,1,0:T(8,128)S(1)} custom-call(f32[4,256,16,128]{3,2,1,0:T(8,128)} %state_hbm.1, f32[256,256]{1,0:T(8,128)S(1)} %bitcast.5, bf16[64,128,128]{2,1,0:T(8,128)(2,1)S(1)} %copy-done, s32[2,128]{1,0:T(2,128)S(1)} %bitcast.6, s32[8,128]{1,0:T(8,128)S(1)} %bitcast.7, bf16[128,256]{1,0:T(8,128)(2,1)S(1)} %copy-done.3, ...), custom_call_target="tpu_custom_call" | custom-call | tf_op jit(solution)/shard_map/exchange/pallas_call | solution.py:713
  79.4 3.7 %place.1 = f32[4,256,16,128]{3,2,1,0:T(8,128)} custom-call(s32[256]{0:T(256)S(1)} %copy-done.4, f32[4,256,16,128]{3,2,1,0:T(8,128)S(1)} %bitcast.4), custom_call_target="tpu_custom_call" | custom-call | tf_op jit(solution)/shard_map/place/pallas_call | solution.py:727
Async XLA Ops:
  0.0 1.6 %copy-start = (bf16[64,128,128]{2,1,0:T(8,128)(2,1)S(1)}, bf16[64,128,128]{2,1,0:T(8,128)(2,1)}, u32[]{:S(2)}) copy-start(bf16[64,128,128]{2,1,0:T(8,128)(2,1)} %inv_hbm.1) | copy-start | bytes 6291460
  1.6 0.9 %copy-start.1 = (f32[16,16,256]{2,1,0:T(8,128)S(1)}, f32[16,16,256]{2,1,0:T(8,128)}, u32[]{:S(2)}) copy-start(f32[16,16,256]{2,1,0:T(8,128)} %param.8) | copy-start | bytes 786436
  2.5 0.9 %copy-start.2 = (bf16[512,256]{1,0:T(8,128)(2,1)S(1)}, bf16[512,256]{1,0:T(8,128)(2,1)}, u32[]{:S(2)}) copy-start(bf16[512,256]{1,0:T(8,128)(2,1)} %constant.5.clone.uptab_ref) | copy-start | bytes 786436
  3.5 0.8 %copy-start.3 = (bf16[128,256]{1,0:T(8,128)(2,1)S(1)}, bf16[128,256]{1,0:T(8,128)(2,1)}, u32[]{:S(2)}) copy-start(bf16[128,256]{1,0:T(8,128)(2,1)} %constant.4.clone.coltab_ref) | copy-start | bytes 196612
  4.3 0.7 copy-start.4
  5.0 0.7 copy-start.5

commit v3 on v2

--- a/solution.py
+++ b/solution.py
@@ -82,7 +82,7 @@
     update = np.zeros((256, 256))
     update[:, :240] = np.einsum("asi,ybr->yabsir", along, along_y).reshape(256, 240)
     up_high, up_low = split_bf16(update)
-    return np.concatenate([col_high, col_low], 0), np.concatenate([up_high, up_low], 0)
+    return np.concatenate([up_high, up_low, col_high, col_low], 0)
 
 
 def iota(shape, dim):
@@ -130,9 +130,9 @@
 
 
 def exchange_kernel(
-    state_hbm, stiff_hbm, inv_hbm, cell_ref, gcol_ref, coltab_ref, uptab_ref,
+    state_hbm, stiff_hbm, inv_hbm, cell_hbm, gcol_hbm, table_hbm,
     dyn,
-    inv, st0, st1, xs, w16, slot_vmem, slots,
+    cell_ref, gcol_ref, table_ref, inv, st0, st1, xs, w16, slot_vmem, slots,
     halo, wv, wq, mid, req, qrow, crow,
     sel, sel_t, place, place_t,
     dyn_high, dyn_low, cols, outb, incb, backb, rcvb, flat, tend, grid, gridb,
@@ -169,6 +169,11 @@
     lax.fori_loop(1, NY, greet_y, 0)
 
 
+    small_copies = []
+    for at, (src, dst) in enumerate(((cell_hbm, cell_ref), (gcol_hbm, gcol_ref))):
+        copy = pltpu.make_async_copy(src, dst, in_sem.at[3 + at])
+        copy.start()
+        small_copies.append(copy)
     stiff_copy = pltpu.make_async_copy(stiff_hbm, xs, in_sem.at[0])
     stiff_copy.start()
     state_copies = []
@@ -185,6 +190,8 @@
 
     inv_copy = pltpu.make_async_copy(inv_hbm, inv, in_sem.at[2])
     inv_copy.start()
+    table_copy = pltpu.make_async_copy(table_hbm, table_ref, in_sem.at[5])
+    table_copy.start()
 
     lane = iota((128, 128), 1)
     sub = iota((128, 128), 0)
@@ -200,6 +207,8 @@
         cell = cell_ref[u : u + 1, :]
         return (((cell >> 7) & 15) * 16 + (cell & 15)).astype(F32)
 
+    for copy in small_copies:
+        copy.wait()
     for v in range(2):
         found = jnp.zeros((128, 128), F32)
         for u in range(2):
@@ -408,8 +417,8 @@
                     low = (total - high.astype(F32)).astype(BF16)
                     dyn_low[y * 16 : y * 16 + 16, f * 128 : f * 128 + 128] = low
                 south, here = here, north
-            main = dot(coltab_ref[...], dyn_high[...])
-            rest = dot(coltab_ref[0:64, :], dyn_low[...])
+            main = dot(table_ref[512:640, :], dyn_high[...])
+            rest = dot(table_ref[512:576, :], dyn_low[...])
             total = main[0:64] + main[64:128] + rest
             cols[pl.ds(x * 64 if fixed else pl.multiple_of(x * 64, 64), 64), :] = total.astype(BF16)
             return carry
@@ -509,21 +518,23 @@
     own_y.start()
     slot_copy.wait()
     halo_copies[0] = send_halo(0)
+    transposed(qrow, place_t)
+    placing()
+    own_y.wait()
+    pltpu.make_async_copy(others_y, others_y, vrecv).wait()
+    selections()
+    take_halo(0, halo_copies[0])
+    table_copy.wait()
+    dynamics(0)
+    forward[0] = permute_and_send(sel, cols, outb, incb, 0, fsend, frecv, 1)
     combine(1)
     halo_copies[1] = send_halo(1)
-    transposed(qrow, place_t)
-    placing()
+    transposed(crow, sel_t)
     grid[...] = jnp.zeros_like(grid)
-    for h in range(NH):
-        take_halo(h, halo_copies[h])
-        dynamics(h)
-        if h == 0:
-            own_y.wait()
-            pltpu.make_async_copy(others_y, others_y, vrecv).wait()
-            selections()
-        forward[h] = permute_and_send(sel, cols, outb, incb, h, fsend, frecv, 1 + h)
-
-    transposed(crow, sel_t)
+    take_halo(1, halo_copies[1])
+    dynamics(1)
+    forward[1] = permute_and_send(sel, cols, outb, incb, 1, fsend, frecv, 2)
+
     inv_copy.wait()
 
     def physics(h):
@@ -554,7 +565,7 @@
         def add(x, carry):
             rows = pl.ds(pl.multiple_of(x * 256, 256), 256)
             near = gridb[pl.ds(pl.multiple_of(x * RX, 16), 256), :]
-            update = dot(uptab_ref[...], near)
+            update = dot(table_ref[0:512, :], near)
             update = update[:256] + update[256:]
             for f in range(2):
                 field = 2 * h + f
@@ -649,6 +660,10 @@
     return pl.BlockSpec(memory_space=pl.ANY)
 
 
+def in_hbm(array):
+    return pltpu.with_memory_space_constraint(array, pltpu.HBM)
+
+
 def hbm_spec():
     return pl.BlockSpec(memory_space=pltpu.HBM)
 
@@ -661,10 +676,13 @@
     return pl.BlockSpec(memory_space=pltpu.SMEM)
 
 
-def per_device(coltab, uptab, state_in, stiffness, elem_cell, group_column, group_inverse):
+def per_device(table, state_in, stiffness, elem_cell, group_column, group_inverse):
     dma = pltpu.SemaphoreType.DMA
     vmem = pltpu.VMEM
     scratch = [
+        vmem((2, 128), I32),
+        vmem((8, 128), I32),
+        vmem((640, 256), BF16),
         vmem((64, LEV, LEV), BF16),
         vmem((2, NE, 16, LEV), F32),
         vmem((2, NE, 16, LEV), F32),
@@ -706,23 +724,23 @@
         vmem((NH, 2, 2, 64, LEV), F32),
         vmem((NH, 2, 2, 64, LEV), F32),
         vmem((NH, 4, 8, LEV), F32),
-        dma((NH, 4)), dma((3,)), dma, dma, dma, dma, dma((5,)),
+        dma((NH, 4)), dma((6,)), dma, dma, dma, dma, dma((5,)),
         dma((NH,)), dma((NH,)), dma((NH,)), dma((NH,)),
         dma((NH, 8)), dma((NH, 8)), dma((NH, 8)), dma((NH, 8)),
     ]
     total = pl.pallas_call(
         exchange_kernel,
         out_shape=jax.ShapeDtypeStruct((4, NE * 16, LEV), F32),
-        in_specs=[any_spec()] * 3 + [vmem_spec()] * 4,
+        in_specs=[any_spec()] * 6,
         out_specs=vmem_spec(),
         scratch_shapes=scratch,
         compiler_params=pltpu.CompilerParams(
-            collective_id=0, has_side_effects=True, vmem_limit_bytes=43 << 20
+            collective_id=0, has_side_effects=True, vmem_limit_bytes=44 << 20
         ),
         name="exchange",
     )(
-        state_in, stiffness.reshape(256, NE), group_inverse, elem_cell.reshape(2, 128),
-        group_column.reshape(8, 128), coltab, uptab,
+        state_in, in_hbm(stiffness.reshape(256, NE)), in_hbm(group_inverse),
+        in_hbm(elem_cell.reshape(2, 128)), in_hbm(group_column.reshape(8, 128)), in_hbm(table),
     )
     return pl.pallas_call(
         place_kernel,
@@ -736,7 +754,7 @@
 
 
 def solution(mesh):
-    coltab, uptab = constant_tables()
+    table = constant_tables()
     placed = (
         P(None, ("gx", "gy"), None, None),
         P(None, None, ("gx", "gy")),
@@ -746,7 +764,7 @@
     )
 
     def run(*args):
-        body = functools.partial(per_device, jnp.asarray(coltab), jnp.asarray(uptab))
+        body = functools.partial(per_device, jnp.asarray(table))
         return jax.shard_map(
             body,
             mesh=mesh,

time: 83.7 us -> 87.6 us (1.047)
  Pallas kernels: 77.5 us -> 87.5 us
  local copies, waits for them, and re-layouts: 5.69 us -> 0.01 us
    pallas_call x1, Pallas kernels: 73.7 us -> 83.7 us  [per_device(): pl.pallas_call(exchange_kernel, out_shape=jax.ShapeDtypeStruct((4, NE * 1...]
    unnamed x12 -> x2, local copies, waits for them, and re-layouts: 5.69 us -> 0.01 us
where the time goes in v3:
time: 87.6 us; the launch traced here: 87.5 us
  Pallas kernels  87.5 us (100%)
    pallas_call x1, Pallas kernels, per_device(): pl.pallas_call(exchange_kernel, out_shape=jax.ShapeDtypeStruct((4, NE * 1...  83.7 us
    pallas_call x1, Pallas kernels, per_device(): pl.pallas_call(place_kernel, out_shape=jax.ShapeDtypeStruct((4, NE, 16, L...  3.73 us

profile of v3, /device:TPU:1, one launch (start us, length us, event | category | flops | bytes accessed | tf_op | source)
XLA Modules:
  0.0 87.5 jit_solution(8017433306393079835)
XLA Ops:
  0.0 0.0 copy-start
  0.0 83.7 %exchange.1 = f32[4,4096,128]{2,1,0:T(8,128)S(1)} custom-call(f32[4,256,16,128]{3,2,1,0:T(8,128)} %state_hbm.1, f32[256,256]{1,0:T(8,128)} %bitcast.6, bf16[64,128,128]{2,1,0:T(8,128)(2,1)} %inv_hbm.1, s32[2,128]{1,0:T(2,128)} %bitcast.5, s32[8,128]{1,0:T(8,128)} %bitcast.7, bf16[640,256]{1,0:T(8,128)(2,1)} %constant.2.clone.table_hbm), custom_call_target="tpu_custom_call" | custom-call | tf_op jit(solution)/shard_map/exchange/pallas_call | solution.py:731
  83.7 0.0 copy-done
  83.7 3.7 %place.1 = f32[4,256,16,128]{3,2,1,0:T(8,128)} custom-call(s32[256]{0:T(256)S(1)} %copy-done, f32[4,256,16,128]{3,2,1,0:T(8,128)S(1)} %bitcast.4), custom_call_target="tpu_custom_call" | custom-call | tf_op jit(solution)/shard_map/place/pallas_call | solution.py:745
Async XLA Ops:
  0.0 83.7 %copy-start = (s32[256]{0:T(256)S(1)}, s32[256]{0:T(256)}, u32[]{:S(2)}) copy-start(s32[256]{0:T(256)} %cell_ref.1) | copy-start | bytes 3076

commit v4 on v1

--- a/solution.py
+++ b/solution.py
@@ -82,7 +82,7 @@
     update = np.zeros((256, 256))
     update[:, :240] = np.einsum("asi,ybr->yabsir", along, along_y).reshape(256, 240)
     up_high, up_low = split_bf16(update)
-    return np.concatenate([col_high, col_low], 0), np.concatenate([up_high, up_low], 0)
+    return np.concatenate([up_high, up_low, col_high, col_low], 0)
 
 
 def iota(shape, dim):
@@ -168,11 +168,11 @@
 
 
 def exchange_kernel(
-    st, cell_ref, gcol_ref, inv, coltab_ref,
-    dyn, gridb,
+    st, cell_ref, gcol_ref, inv, table_ref,
+    dyn,
     halo, wv, wq, mid, req, qrow, crow,
     sel, sel_t, place, place_t,
-    dyn_high, dyn_low, cols, outb, incb, backb, rcvb, flat, tend, grid,
+    dyn_high, dyn_low, cols, outb, incb, backb, rcvb, flat, tend, grid, gridb,
     sx, sy, sc, rx, ry, rc,
     tx, ty, tc, ux, uy, uc,
     wsend, wrecv, vsend, vrecv, loc_sem,
@@ -369,8 +369,8 @@
                     low = (total - high.astype(F32)).astype(BF16)
                     dyn_low[y * 16 : y * 16 + 16, f * 128 : f * 128 + 128] = low
                 south, here = here, north
-            main = dot(coltab_ref[...], dyn_high[...])
-            rest = dot(coltab_ref[0:64, :], dyn_low[...])
+            main = dot(table_ref[512:640, :], dyn_high[...])
+            rest = dot(table_ref[512:576, :], dyn_low[...])
             total = main[0:64] + main[64:128] + rest
             cols[pl.ds(x * 64 if fixed else pl.multiple_of(x * 64, 64), 64), :] = total.astype(BF16)
             return carry
@@ -464,13 +464,16 @@
         lax.fori_loop(0, 8, step, 0)
 
     halo_copies, forward, back_copies = [None] * NH, [None] * NH, [None] * NH
-    halo_copies[0] = send_halo(0)
+    for h in range(NH):
+        halo_copies[h] = send_halo(h)
+    transposed(qrow, place_t)
+    placing()
+    grid[...] = jnp.zeros_like(grid)
     own_x.wait()
     pltpu.make_async_copy(others_x, others_x, wrecv).wait()
     lax.fori_loop(1, NY, ask_y, 0)
     own_y = pltpu.make_async_copy(mid.at[:, gy], req.at[:, gy], loc_sem.at[0])
     own_y.start()
-    halo_copies[1] = send_halo(1)
     for h in range(NH):
         take_halo(h, halo_copies[h])
         dynamics(h)
@@ -479,9 +482,6 @@
             pltpu.make_async_copy(others_y, others_y, vrecv).wait()
             selections()
         forward[h] = permute_and_send(sel, cols, outb, incb, h, fsend, frecv, 1 + h)
-        if h == 0:
-            transposed(qrow, place_t)
-            placing()
 
     transposed(crow, sel_t)
 
@@ -507,8 +507,21 @@
         physics(h)
         back_copies[h] = permute_and_send(place_t, tend, backb, rcvb, h, bsend, brecv, 3 + h)
 
-    grid[...] = jnp.zeros_like(grid)
     ring_copies = []
+
+    def finish(h):
+        def add(x, carry):
+            rows = pl.ds(pl.multiple_of(x * 256, 256), 256)
+            near = gridb[pl.ds(pl.multiple_of(x * RX, 16), 256), :]
+            update = dot(table_ref[0:512, :], near)
+            update = update[:256] + update[256:]
+            for f in range(2):
+                field = 2 * h + f
+                dyn[field, rows, :] = dyn[field, rows, :] + update[:, f * LEV : (f + 1) * LEV]
+            return carry
+
+        lax.fori_loop(0, TX, add, 0)
+
     for h in range(NH):
         back_copies[h].wait()
         wait_all(rcvb, h, brecv)
@@ -550,9 +563,7 @@
         for copy in copies:
             copy.start()
         ring_copies.append(copies)
-
-    for h in range(NH):
-        for copy in ring_copies[h]:
+        for copy in copies:
             copy.wait_recv()
         for u in range(2):
             for i in range(2):
@@ -567,7 +578,9 @@
                 for i in range(2):
                     to = big_x * RX + i * 40 + base
                     grid[h, u, to : to + 2, :] = uc[h, at, u * 4 + i * 2 : u * 4 + i * 2 + 2, :]
-            gridb[h, :, u * 128 : (u + 1) * 128] = grid[h, u].astype(BF16)
+            gridb[:, u * 128 : (u + 1) * 128] = grid[h, u].astype(BF16)
+        finish(h)
+
 
     pltpu.make_async_copy(others_x, others_x, wsend).wait()
     pltpu.make_async_copy(others_y, others_y, vsend).wait()
@@ -578,46 +591,25 @@
             copy.wait_send()
 
 
-def finish_kernel(cell_ref, ret, table_ref, dyn, out_hbm, total, outv, out_sem):
-    def add(x, carry):
-        rows = pl.ds(pl.multiple_of(x * 256, 256), 256)
-        for h in range(NH):
-            near = ret[h, pl.ds(pl.multiple_of(x * RX, 16), 256), :]
-            update = dot(table_ref[...], near)
-            update = update[:256] + update[256:]
-            for f in range(2):
-                field = 2 * h + f
-                total[field, rows, :] = dyn[field, rows, :] + update[:, f * 128 : (f + 1) * 128]
+def place_kernel(cell_ref, total, out_hbm, sem):
+    def step(s, carry):
+        for k in range(8):
+            at = s * 8 + k
+            cell = cell_ref[at]
+            tile = ((cell >> 7) & 15) * 16 + (cell & 15)
+            pltpu.make_async_copy(total.at[:, tile], out_hbm.at[:, at], sem).start()
         return carry
 
-    lax.fori_loop(0, TX, add, 0)
-
-    def gather(s, carry):
-        cell = cell_ref[s]
-        tile = ((cell >> 7) & 15) * 16 + (cell & 15)
-        source = pl.ds(pl.multiple_of(tile * 16, 16), 16)
-        target = pl.ds(pl.multiple_of(s * 16, 16), 16)
-        for field in range(4):
-            outv[field, target, :] = total[field, source, :]
-        return carry
-
-    stores = []
-    for part in range(8):
-        lax.fori_loop(part * 32, part * 32 + 32, gather, 0, unroll=4)
-        rows = pl.ds(part * 512, 512)
-        copy = pltpu.make_async_copy(outv.at[:, rows], out_hbm.at[:, rows], out_sem.at[part])
-        copy.start()
-        stores.append(copy)
-    for copy in stores:
-        copy.wait()
+    lax.fori_loop(0, NE // 8, step, 0)
+    pltpu.make_async_copy(total, out_hbm, sem).wait()
 
 
 def any_spec():
     return pl.BlockSpec(memory_space=pl.ANY)
 
 
-def hbm_spec():
-    return pl.BlockSpec(memory_space=pltpu.HBM)
+def in_hbm(array):
+    return pltpu.with_memory_space_constraint(array, pltpu.HBM)
 
 
 def vmem_spec():
@@ -628,7 +620,7 @@
     return pl.BlockSpec(memory_space=pltpu.SMEM)
 
 
-def per_device(coltab, uptab, state_in, stiffness, elem_cell, group_column, group_inverse):
+def per_device(table, state_in, stiffness, elem_cell, group_column, group_inverse):
     state = state_in.reshape(4, NE * 16, LEV)
     dma = pltpu.SemaphoreType.DMA
     vmem = pltpu.VMEM
@@ -636,7 +628,7 @@
     combined = pl.pallas_call(
         combine_kernel,
         out_shape=whole,
-        in_specs=[smem_spec(), hbm_spec(), hbm_spec()],
+        in_specs=[smem_spec(), any_spec(), any_spec()],
         out_specs=vmem_spec(),
         scratch_shapes=[
             vmem((4, NE * 16, LEV), F32),
@@ -645,9 +637,9 @@
             dma,
             dma((8,)),
         ],
-        compiler_params=pltpu.CompilerParams(vmem_limit_bytes=42 << 20),
+        compiler_params=pltpu.CompilerParams(vmem_limit_bytes=30 << 20),
         name="combine",
-    )(elem_cell, state, stiffness.reshape(256, NE))
+    )(elem_cell, in_hbm(state), in_hbm(stiffness.reshape(256, NE)))
     scratch = [
         vmem((4, NHALO * 16, LEV), F32),
         vmem((128, 128), F32),
@@ -670,6 +662,7 @@
         vmem((NC, 256), BF16),
         vmem((NC, 256), BF16),
         vmem((NH, 2, RROWS, LEV), F32),
+        vmem((RROWS, 256), BF16),
         vmem((NH, 2, 2, 64, LEV), F32),
         vmem((NH, 2, 2, 64, LEV), F32),
         vmem((NH, 4, 8, LEV), F32),
@@ -686,31 +679,30 @@
         dma((NH,)), dma((NH,)), dma((NH,)), dma((NH,)),
         dma((NH, 8)), dma((NH, 8)), dma((NH, 8)), dma((NH, 8)),
     ]
-    dyn, ret = pl.pallas_call(
+    total = pl.pallas_call(
         exchange_kernel,
-        out_shape=(whole, jax.ShapeDtypeStruct((NH, RROWS, 256), BF16)),
+        out_shape=whole,
         in_specs=[vmem_spec()] * 5,
-        out_specs=(vmem_spec(), vmem_spec()),
+        out_specs=vmem_spec(),
         scratch_shapes=scratch,
         compiler_params=pltpu.CompilerParams(
             collective_id=0, has_side_effects=True, vmem_limit_bytes=28 << 20
         ),
         name="exchange",
-    )(combined, elem_cell.reshape(2, 128), group_column.reshape(8, 128), group_inverse, coltab)
-    out = pl.pallas_call(
-        finish_kernel,
-        out_shape=whole,
-        in_specs=[smem_spec(), vmem_spec(), vmem_spec(), vmem_spec()],
+    )(combined, elem_cell.reshape(2, 128), group_column.reshape(8, 128), group_inverse, table)
+    return pl.pallas_call(
+        place_kernel,
+        out_shape=jax.ShapeDtypeStruct((4, NE, 16, LEV), F32),
+        in_specs=[smem_spec(), vmem_spec()],
         out_specs=any_spec(),
-        scratch_shapes=[vmem((4, NE * 16, LEV), F32), vmem((4, NE * 16, LEV), F32), dma((8,))],
-        compiler_params=pltpu.CompilerParams(vmem_limit_bytes=32 << 20),
-        name="finish",
-    )(elem_cell, ret, uptab, dyn)
-    return out.reshape(4, NE, 16, LEV)
+        scratch_shapes=[dma],
+        compiler_params=pltpu.CompilerParams(vmem_limit_bytes=4 << 20),
+        name="place",
+    )(elem_cell, total.reshape(4, NE, 16, LEV))
 
 
 def solution(mesh):
-    coltab, uptab = constant_tables()
+    table = constant_tables()
     placed = (
         P(None, ("gx", "gy"), None, None),
         P(None, None, ("gx", "gy")),
@@ -720,7 +712,7 @@
     )
 
     def run(*args):
-        body = functools.partial(per_device, jnp.asarray(coltab), jnp.asarray(uptab))
+        body = functools.partial(per_device, jnp.asarray(table))
         return jax.shard_map(
             body,
             mesh=mesh,

time: 78.6 us -> 82.5 us (1.050)
  Pallas kernels: 76.7 us -> 81.5 us
  local copies, waits for them, and re-layouts: 1.65 us -> 0.69 us
    pallas_call x3, Pallas kernels: 76.7 us -> 81.5 us  [the longest x1 68.4 us: per_device(): pl.pallas_call(exchange_kernel, out_shape=whole, in_specs=[vmem_spec()] *...]
    unnamed x12 -> x8, local copies, waits for them, and re-layouts: 1.65 us -> 0.69 us
where the time goes in v4:
time: 82.5 us; the launch traced here: 82.3 us
  Pallas kernels  81.5 us (99%)
    pallas_call x1, Pallas kernels, per_device(): pl.pallas_call(exchange_kernel, out_shape=whole, in_specs=[vmem_spec()] *...  68.4 us
    pallas_call x1, Pallas kernels, per_device(): pl.pallas_call(combine_kernel, out_shape=whole, in_specs=[smem_spec(), an...  9.41 us
    pallas_call x1, Pallas kernels, per_device(): pl.pallas_call(place_kernel, out_shape=jax.ShapeDtypeStruct((4, NE, 16, L...  3.73 us

profile of v4, /device:TPU:1, one launch (start us, length us, event | category | flops | bytes accessed | tf_op | source)
XLA Modules:
  0.0 82.3 jit_solution(593187560246200840)
XLA Ops:
  0.0 0.0 copy-start.2
  0.0 0.7 copy-done.2
  0.7 0.0 copy-start
  0.7 0.0 copy-start.1
  0.7 0.0 copy-start.3
  0.7 9.4 %combine.1.st = f32[4,4096,128]{2,1,0:T(8,128)S(1)} custom-call(s32[256]{0:T(256)S(1)} %copy-done.2, f32[4,4096,128]{2,1,0:T(8,128)} %bitcast.8, f32[256,256]{1,0:T(8,128)} %bitcast.9), custom_call_target="tpu_custom_call" | custom-call | tf_op jit(solution)/shard_map/combine/pallas_call | solution.py:628
  10.1 0.0 copy-done
  10.1 0.0 copy-done.1
  10.1 0.0 copy-done.3
  10.1 68.4 %exchange.1 = f32[4,4096,128]{2,1,0:T(8,128)S(1)} custom-call(f32[4,4096,128]{2,1,0:T(8,128)S(1)} %combine.1.st, s32[2,128]{1,0:T(2,128)S(1)} %bitcast.6, s32[8,128]{1,0:T(8,128)S(1)} %bitcast.7, bf16[64,128,128]{2,1,0:T(8,128)(2,1)S(1)} %copy-done, bf16[640,256]{1,0:T(8,128)(2,1)S(1)} %copy-done.1), custom_call_target="tpu_custom_call" | custom-call | tf_op jit(solution)/shard_map/exchange/pallas_call | solution.py:682
  78.5 3.7 %place.1 = f32[4,256,16,128]{3,2,1,0:T(8,128)} custom-call(s32[256]{0:T(256)S(1)} %copy-done.2, f32[4,256,16,128]{3,2,1,0:T(8,128)S(1)} %bitcast.5), custom_call_target="tpu_custom_call" | custom-call | tf_op jit(solution)/shard_map/place/pallas_call | solution.py:693
Async XLA Ops:
  0.0 0.7 copy-start.2
  0.7 9.4 %copy-start = (bf16[64,128,128]{2,1,0:T(8,128)(2,1)S(1)}, bf16[64,128,128]{2,1,0:T(8,128)(2,1)}, u32[]{:S(2)}) copy-start(bf16[64,128,128]{2,1,0:T(8,128)(2,1)} %inv.1) | copy-start | bytes 6291460
  0.7 9.4 %copy-start.1 = (bf16[640,256]{1,0:T(8,128)(2,1)S(1)}, bf16[640,256]{1,0:T(8,128)(2,1)}, u32[]{:S(2)}) copy-start(bf16[640,256]{1,0:T(8,128)(2,1)} %constant.2.clone.table_ref) | copy-start | bytes 983044
  0.7 9.4 %copy-start.3 = (s32[1024]{0:T(1024)S(1)}, s32[1024]{0:T(1024)}, u32[]{:S(2)}) copy-start(s32[1024]{0:T(1024)} %param.9) | copy-start | bytes 12292

commit v5 on v4

--- a/solution.py
+++ b/solution.py
@@ -563,7 +563,9 @@
         for copy in copies:
             copy.start()
         ring_copies.append(copies)
-        for copy in copies:
+
+    for h in range(NH):
+        for copy in ring_copies[h]:
             copy.wait_recv()
         for u in range(2):
             for i in range(2):
@@ -639,7 +641,7 @@
         ],
         compiler_params=pltpu.CompilerParams(vmem_limit_bytes=30 << 20),
         name="combine",
-    )(elem_cell, in_hbm(state), in_hbm(stiffness.reshape(256, NE)))
+    )(elem_cell, in_hbm(state), stiffness.reshape(256, NE))
     scratch = [
         vmem((4, NHALO * 16, LEV), F32),
         vmem((128, 128), F32),

time: 82.5 us -> 75.4 us (0.914)
  Pallas kernels: 81.5 us -> 73.3 us
  local copies, waits for them, and re-layouts: 0.69 us -> 1.64 us
    pallas_call x1, Pallas kernels: 68.4 us -> 63.4 us  [per_device(): pl.pallas_call(exchange_kernel, out_shape=whole, in_specs=[vmem_spec()] *...]
    pallas_call x1, Pallas kernels: 9.41 us -> 6.13 us  [per_device(): pl.pallas_call(combine_kernel, out_shape=whole, in_specs=[smem_spec(), an...]
    unnamed x8 -> x10, local copies, waits for them, and re-layouts: 0.69 us -> 1.64 us
where the time goes in v5:
time: 75.4 us; the launch traced here: 75 us
  Pallas kernels  73.3 us (97%)
  local copies, waits for them, and re-layouts  1.64 us (2%)
    pallas_call x1, Pallas kernels, per_device(): pl.pallas_call(exchange_kernel, out_shape=whole, in_specs=[vmem_spec()] *...  63.4 us
    pallas_call x1, Pallas kernels, per_device(): pl.pallas_call(combine_kernel, out_shape=whole, in_specs=[smem_spec(), an...  6.13 us
    pallas_call x1, Pallas kernels, per_device(): pl.pallas_call(place_kernel, out_shape=jax.ShapeDtypeStruct((4, NE, 16, L...  3.73 us
    unnamed x10, local copies, waits for them, and re-layouts  1.64 us

profile of v5, /device:TPU:1, one launch (start us, length us, event | category | flops | bytes accessed | tf_op | source)
XLA Modules:
  0.0 75.0 jit_solution(13096585335724393409)
XLA Ops:
  0.0 0.0 copy-start.2
  0.0 0.9 %copy-done.2 = f32[16,16,256]{2,1,0:T(8,128)S(1)} copy-done((f32[16,16,256]{2,1,0:T(8,128)S(1)}, f32[16,16,256]{2,1,0:T(8,128)}, u32[]{:S(2)}) %copy-start.2) | copy-done | bytes 262168
  1.0 0.0 copy-start.3
  1.0 0.7 copy-done.3
  1.6 0.0 copy-start
  1.6 0.0 copy-start.1
  1.6 0.0 copy-start.4
  1.6 6.1 %combine.1.st = f32[4,4096,128]{2,1,0:T(8,128)S(1)} custom-call(s32[256]{0:T(256)S(1)} %copy-done.3, f32[4,4096,128]{2,1,0:T(8,128)} %bitcast.9, f32[256,256]{1,0:T(8,128)S(1)} %bitcast.6), custom_call_target="tpu_custom_call" | custom-call | tf_op jit(solution)/shard_map/combine/pallas_call | solution.py:630
  7.8 0.0 copy-done
  7.8 0.0 copy-done.1
  7.8 0.0 copy-done.4
  7.8 63.4 %exchange.1 = f32[4,4096,128]{2,1,0:T(8,128)S(1)} custom-call(f32[4,4096,128]{2,1,0:T(8,128)S(1)} %combine.1.st, s32[2,128]{1,0:T(2,128)S(1)} %bitcast.7, s32[8,128]{1,0:T(8,128)S(1)} %bitcast.8, bf16[64,128,128]{2,1,0:T(8,128)(2,1)S(1)} %copy-done, bf16[640,256]{1,0:T(8,128)(2,1)S(1)} %copy-done.1), custom_call_target="tpu_custom_call" | custom-call | tf_op jit(solution)/shard_map/exchange/pallas_call | solution.py:684
  71.2 3.7 %place.1 = f32[4,256,16,128]{3,2,1,0:T(8,128)} custom-call(s32[256]{0:T(256)S(1)} %copy-done.3, f32[4,256,16,128]{3,2,1,0:T(8,128)S(1)} %bitcast.5), custom_call_target="tpu_custom_call" | custom-call | tf_op jit(solution)/shard_map/place/pallas_call | solution.py:695
Async XLA Ops:
  0.0 0.9 %copy-start.2 = (f32[16,16,256]{2,1,0:T(8,128)S(1)}, f32[16,16,256]{2,1,0:T(8,128)}, u32[]{:S(2)}) copy-start(f32[16,16,256]{2,1,0:T(8,128)} %param.7) | copy-start | bytes 786436
  1.0 0.7 copy-start.3
  1.6 6.1 %copy-start = (bf16[64,128,128]{2,1,0:T(8,128)(2,1)S(1)}, bf16[64,128,128]{2,1,0:T(8,128)(2,1)}, u32[]{:S(2)}) copy-start(bf16[64,128,128]{2,1,0:T(8,128)(2,1)} %inv.1) | copy-start | bytes 6291460
  1.6 6.2 %copy-start.1 = (bf16[640,256]{1,0:T(8,128)(2,1)S(1)}, bf16[640,256]{1,0:T(8,128)(2,1)}, u32[]{:S(2)}) copy-start(bf16[640,256]{1,0:T(8,128)(2,1)} %constant.2.clone.table_ref) | copy-start | bytes 983044
  1.6 6.2 %copy-start.4 = (s32[1024]{0:T(1024)S(1)}, s32[1024]{0:T(1024)}, u32[]{:S(2)}) copy-start(s32[1024]{0:T(1024)} %param.9) | copy-start | bytes 12292

commit v6 on v5

--- a/solution.py
+++ b/solution.py
@@ -129,7 +129,13 @@
         return b * 32 + d * 8 + a * 2 + c
 
 
-def combine_kernel(cell_ref, state_hbm, stiff_hbm, out_ref, st, xs, w, stiff_sem, state_sem):
+def combine_kernel(
+    cell_ref, gcol_hbm, state_hbm, stiff_hbm,
+    out_ref, wq, rank_ref,
+    st, xs, w, wv, gcol_ref, stiff_sem, gcol_sem, state_sem,
+):
+    gcol_copy = pltpu.make_async_copy(gcol_hbm, gcol_ref, gcol_sem)
+    gcol_copy.start()
     stiff_copy = pltpu.make_async_copy(stiff_hbm, xs, stiff_sem)
     stiff_copy.start()
     loads = []
@@ -149,6 +155,39 @@
         for u in range(2):
             w[u, pl.ds(n, 256, stride=16), :] = block[:, u * 128 : (u + 1) * 128]
 
+    lane, sub = iota((128, 128), 1), iota((128, 128), 0)
+    gcol_copy.wait()
+
+    upper = jnp.where(sub < lane, 1.0, 0.0).astype(BF16)
+    seen = jnp.zeros((128, 1), F32)
+    want_high = jnp.zeros((128, 128), F32)
+    want_low = jnp.zeros((128, 128), F32)
+    for block in range(8):
+        named = gcol_ref[block : block + 1, :]
+        source, local = named >> 10, named & 1023
+        hit = jnp.broadcast_to(source, (128, 128)) == sub
+        onehot = jnp.where(hit, 1.0, 0.0)
+        before = dot(onehot.astype(BF16), upper) + seen
+        seen = seen + jnp.sum(onehot, axis=1, keepdims=True)
+        rank = jnp.sum(jnp.where(hit, before, 0.0), axis=0, keepdims=True)
+        rank_ref[block : block + 1, :] = rank
+        ranked = jnp.broadcast_to(rank, (128, 128)) == sub.astype(F32)
+        high = (local >> 5).astype(F32)
+        low = (local & 31).astype(F32)
+        zero = jnp.zeros((128, 128), F32)
+        chosen_high = jnp.where(ranked, jnp.broadcast_to(high, (128, 128)), zero).astype(BF16)
+        chosen_low = jnp.where(ranked, jnp.broadcast_to(low, (128, 128)), zero).astype(BF16)
+        onehot = onehot.astype(BF16)
+        want_high = want_high + dot_nt(onehot, chosen_high)
+        want_low = want_low + dot_nt(onehot, chosen_low)
+    wv[...] = want_high * 32.0 + want_low
+
+    def row_out(s, carry):
+        for y in range(NY):
+            wq[s, y] = wv[pl.ds(s * NY + y, 1), :]
+        return carry
+
+    lax.fori_loop(0, NX, row_out, 0)
     def step(g, carry):
         rows = pl.ds(pl.multiple_of(g * 256, 256), 256)
         state = jnp.concatenate([st[f, rows, :] for f in range(4)], axis=1)
@@ -168,9 +207,9 @@
 
 
 def exchange_kernel(
-    st, cell_ref, gcol_ref, inv, table_ref,
+    st, cell_ref, gcol_ref, rank_ref, wq, inv, table_ref,
     dyn,
-    halo, wv, wq, mid, req, qrow, crow,
+    halo, mid, req, qrow, crow,
     sel, sel_t, place, place_t,
     dyn_high, dyn_low, cols, outb, incb, backb, rcvb, flat, tend, grid, gridb,
     sx, sy, sc, rx, ry, rc,
@@ -215,36 +254,8 @@
     def to_row(col):
         return jnp.sum(jnp.where(eye, jnp.broadcast_to(col, (128, 128)), 0.0), axis=0, keepdims=True)
 
-    upper = jnp.where(sub < lane, 1.0, 0.0).astype(BF16)
-    seen = jnp.zeros((128, 1), F32)
-    want_high = jnp.zeros((128, 128), F32)
-    want_low = jnp.zeros((128, 128), F32)
-    for block in range(8):
-        named = gcol_ref[block : block + 1, :]
-        source, local = named >> 10, named & 1023
-        hit = jnp.broadcast_to(source, (128, 128)) == sub
-        onehot = jnp.where(hit, 1.0, 0.0)
-        before = dot(onehot.astype(BF16), upper) + seen
-        seen = seen + jnp.sum(onehot, axis=1, keepdims=True)
-        rank = jnp.sum(jnp.where(hit, before, 0.0), axis=0, keepdims=True)
-        qrow[block : block + 1, :] = peers.position(source).astype(F32) * 8.0 + rank
-        ranked = jnp.broadcast_to(rank, (128, 128)) == sub.astype(F32)
-        high = (local >> 5).astype(F32)
-        low = (local & 31).astype(F32)
-        zero = jnp.zeros((128, 128), F32)
-        chosen_high = jnp.where(ranked, jnp.broadcast_to(high, (128, 128)), zero).astype(BF16)
-        chosen_low = jnp.where(ranked, jnp.broadcast_to(low, (128, 128)), zero).astype(BF16)
-        onehot = onehot.astype(BF16)
-        want_high = want_high + dot_nt(onehot, chosen_high)
-        want_low = want_low + dot_nt(onehot, chosen_low)
-    wv[...] = want_high * 32.0 + want_low
-
-    def row_out(s, carry):
-        for y in range(NY):
-            wq[s, y] = wv[pl.ds(s * NY + y, 1), :]
-        return carry
-
-    lax.fori_loop(0, NX, row_out, 0)
+    source = gcol_ref[...] >> 10
+    qrow[...] = peers.position(source).astype(F32) * 8.0 + rank_ref[...]
     pl.semaphore_wait(barrier, NX + NY - 2 + len(CORNERS))
 
     def ask_x(k, carry):
@@ -627,25 +638,31 @@
     dma = pltpu.SemaphoreType.DMA
     vmem = pltpu.VMEM
     whole = jax.ShapeDtypeStruct((4, NE * 16, LEV), F32)
-    combined = pl.pallas_call(
+    named = group_column.reshape(8, 128)
+    combined, wanted, rank = pl.pallas_call(
         combine_kernel,
-        out_shape=whole,
-        in_specs=[smem_spec(), any_spec(), any_spec()],
-        out_specs=vmem_spec(),
+        out_shape=(
+            whole,
+            jax.ShapeDtypeStruct((NX, NY, 1, 128), F32),
+            jax.ShapeDtypeStruct((8, 128), F32),
+        ),
+        in_specs=[smem_spec(), any_spec(), any_spec(), any_spec()],
+        out_specs=(vmem_spec(), vmem_spec(), vmem_spec()),
         scratch_shapes=[
             vmem((4, NE * 16, LEV), F32),
             vmem((256, 256), F32),
             vmem((2, NE * 16, LEV), F32),
+            vmem((128, 128), F32),
+            vmem((8, 128), I32),
+            dma,
             dma,
             dma((8,)),
         ],
         compiler_params=pltpu.CompilerParams(vmem_limit_bytes=30 << 20),
         name="combine",
-    )(elem_cell, in_hbm(state), stiffness.reshape(256, NE))
+    )(elem_cell, in_hbm(named), in_hbm(state), stiffness.reshape(256, NE))
     scratch = [
         vmem((4, NHALO * 16, LEV), F32),
-        vmem((128, 128), F32),
-        vmem((NX, NY, 1, 128), F32),
         vmem((NX, NY, 1, 128), F32),
         vmem((NX, NY, 1, 128), F32),
         vmem((8, 128), F32),
@@ -684,14 +701,14 @@
     total = pl.pallas_call(
         exchange_kernel,
         out_shape=whole,
-        in_specs=[vmem_spec()] * 5,
+        in_specs=[vmem_spec()] * 7,
         out_specs=vmem_spec(),
         scratch_shapes=scratch,
         compiler_params=pltpu.CompilerParams(
             collective_id=0, has_side_effects=True, vmem_limit_bytes=28 << 20
         ),
         name="exchange",
-    )(combined, elem_cell.reshape(2, 128), group_column.reshape(8, 128), group_inverse, table)
+    )(combined, elem_cell.reshape(2, 128), named, rank, wanted, group_inverse, table)
     return pl.pallas_call(
         place_kernel,
         out_shape=jax.ShapeDtypeStruct((4, NE, 16, LEV), F32),

time: 75.4 us -> 77.3 us (1.025)
  Pallas kernels: 73.3 us -> 74.9 us
    pallas_call x1, Pallas kernels: 6.13 us -> 7.85 us  [per_device(): pl.pallas_call(combine_kernel, out_shape=(whole, jax.ShapeDtypeStruct((NX...]
where the time goes in v6:
time: 77.3 us; the launch traced here: 76.8 us
  Pallas kernels  74.9 us (97%)
  local copies, waits for them, and re-layouts  1.79 us (2%)
    pallas_call x1, Pallas kernels, per_device(): pl.pallas_call(exchange_kernel, out_shape=whole, in_specs=[vmem_spec()] *...  63.3 us
    pallas_call x1, Pallas kernels, per_device(): pl.pallas_call(combine_kernel, out_shape=(whole, jax.ShapeDtypeStruct((NX...  7.85 us
    pallas_call x1, Pallas kernels, per_device(): pl.pallas_call(place_kernel, out_shape=jax.ShapeDtypeStruct((4, NE, 16, L...  3.73 us
    unnamed x10, local copies, waits for them, and re-layouts  1.79 us

profile of v6, /device:TPU:1, one launch (start us, length us, event | category | flops | bytes accessed | tf_op | source)
XLA Modules:
  0.0 76.8 jit_solution(5219152270136801987)
XLA Ops:
  0.0 0.0 copy-start.1
  0.0 0.0 copy-start
  0.0 0.0 copy-start.2
  0.0 1.1 %copy-done.2 = f32[16,16,256]{2,1,0:T(8,128)S(1)} copy-done((f32[16,16,256]{2,1,0:T(8,128)S(1)}, f32[16,16,256]{2,1,0:T(8,128)}, u32[]{:S(2)}) %copy-start.2) | copy-done | bytes 262168
  1.1 0.0 copy-start.4
  1.1 0.7 copy-done.4
  1.8 0.0 copy-start.3
  1.8 7.8 %combine.1 = (f32[4,4096,128]{2,1,0:T(8,128)S(1)}, f32[16,8,1,128]{3,2,1,0:T(1,128)S(1)}, f32[8,128]{1,0:T(8,128)S(1)}) custom-call(s32[256]{0:T(256)S(1)} %copy-done.4, s32[8,128]{1,0:T(8,128)} %bitcast.7, f32[4,4096,128]{2,1,0:T(8,128)} %bitcast.10, f32[256,256]{1,0:T(8,128)S(1)} %bitcast.6), custom_call_target="tpu_custom_call" | custom-call | tf_op jit(solution)/shard_map/combine/pallas_call | solution.py:642
  9.6 0.0 copy-done.1
  9.7 0.0 copy-done
  9.7 0.0 copy-done.3
  9.7 63.3 %exchange.1 = f32[4,4096,128]{2,1,0:T(8,128)S(1)} custom-call(f32[4,4096,128]{2,1,0:T(8,128)S(1)} %get-tuple-element.8.st, s32[2,128]{1,0:T(2,128)S(1)} %bitcast.9, s32[8,128]{1,0:T(8,128)S(1)} %bitcast.8, f32[8,128]{1,0:T(8,128)S(1)} %get-tuple-element.9.rank_ref, f32[16,8,1,128]{3,2,1,0:T(1,128)S(1)} %get-tuple-element.10.wq, ...), custom_call_target="tpu_custom_call" | custom-call | tf_op jit(solution)/shard_map/exchange/pallas_call | solution.py:701
  73.0 3.7 %place.1 = f32[4,256,16,128]{3,2,1,0:T(8,128)} custom-call(s32[256]{0:T(256)S(1)} %copy-done.4, f32[4,256,16,128]{3,2,1,0:T(8,128)S(1)} %bitcast.5), custom_call_target="tpu_custom_call" | custom-call | tf_op jit(solution)/shard_map/place/pallas_call | solution.py:712
Async XLA Ops:
  0.0 9.6 %copy-start.1 = (bf16[640,256]{1,0:T(8,128)(2,1)S(1)}, bf16[640,256]{1,0:T(8,128)(2,1)}, u32[]{:S(2)}) copy-start(bf16[640,256]{1,0:T(8,128)(2,1)} %constant.2.clone.table_ref) | copy-start | bytes 983044
  0.0 9.6 %copy-start = (bf16[64,128,128]{2,1,0:T(8,128)(2,1)S(1)}, bf16[64,128,128]{2,1,0:T(8,128)(2,1)}, u32[]{:S(2)}) copy-start(bf16[64,128,128]{2,1,0:T(8,128)(2,1)} %inv.1) | copy-start | bytes 6291460
  0.0 1.1 %copy-start.2 = (f32[16,16,256]{2,1,0:T(8,128)S(1)}, f32[16,16,256]{2,1,0:T(8,128)}, u32[]{:S(2)}) copy-start(f32[16,16,256]{2,1,0:T(8,128)} %param.7) | copy-start | bytes 786436
  1.1 0.7 copy-start.4
  1.8 7.9 %copy-start.3 = (s32[1024]{0:T(1024)S(1)}, s32[1024]{0:T(1024)}, u32[]{:S(2)}) copy-start(s32[1024]{0:T(1024)} %param.9) | copy-start | bytes 12292

commit v7 on v5

--- a/solution.py
+++ b/solution.py
@@ -170,40 +170,32 @@
 def exchange_kernel(
     st, cell_ref, gcol_ref, inv, table_ref,
     dyn,
-    halo, wv, wq, mid, req, qrow, crow,
+    halo, wv, wq, req, qrow, crow,
     sel, sel_t, place, place_t,
     dyn_high, dyn_low, cols, outb, incb, backb, rcvb, flat, tend, grid, gridb,
     sx, sy, sc, rx, ry, rc,
     tx, ty, tc, ux, uy, uc,
-    wsend, wrecv, vsend, vrecv, loc_sem,
+    wsend, wrecv, loc_sem,
     fsend, frecv, bsend, brecv, hsend, hrecv, gsend, grecv,
 ):
     gx, gy = lax.axis_index("gx"), lax.axis_index("gy")
+    me = gx * NY + gy
     peers = Peers(gx, gy)
     barrier = pltpu.get_barrier_semaphore()
 
-    def other_x(k):
-        return lax.rem(gx + k, NX)
-
-    def other_y(k):
-        return lax.rem(gy + k, NY)
-
-    for dgx, dgy, _, _, _, _ in CORNERS:
-        pl.semaphore_signal(
-            barrier, inc=1, device_id=(other_x(NX + dgx), other_y(NY + dgy)), device_id_type=MESH
-        )
-
-    def greet_x(k, carry):
-        pl.semaphore_signal(barrier, inc=1, device_id=(other_x(k), gy), device_id_type=MESH)
-        return carry
-
-    def greet_y(k, carry):
-        pl.semaphore_signal(barrier, inc=1, device_id=(gx, other_y(k)), device_id_type=MESH)
-        return carry
-
-    lax.fori_loop(1, NX, greet_x, 0)
-    lax.fori_loop(1, NY, greet_y, 0)
-
+    def to_peers(act):
+        def step(b, carry):
+            for tgx, tgy, _, _ in peers.block(b):
+                act(tgx, tgy)
+            return carry
+
+        step(0, 0)
+        lax.fori_loop(1, 4, step, 0)
+
+    def greet(tgx, tgy):
+        pl.semaphore_signal(barrier, inc=1, device_id=(tgx, tgy), device_id_type=MESH)
+
+    to_peers(greet)
 
     lane = iota((128, 128), 1)
     sub = iota((128, 128), 0)
@@ -241,32 +233,22 @@
 
     def row_out(s, carry):
         for y in range(NY):
-            wq[s, y] = wv[pl.ds(s * NY + y, 1), :]
+            wq[s * NY + y] = wv[pl.ds(s * NY + y, 1), :]
         return carry
 
     lax.fori_loop(0, NX, row_out, 0)
-    pl.semaphore_wait(barrier, NX + NY - 2 + len(CORNERS))
-
-    def ask_x(k, carry):
+    pl.semaphore_wait(barrier, ND - 1)
+
+    def ask(tgx, tgy):
         pltpu.make_async_remote_copy(
-            wq.at[other_x(k)], mid.at[gx], wsend, wrecv,
-            device_id=(other_x(k), gy), device_id_type=MESH,
+            wq.at[tgx * NY + tgy], req.at[me], wsend, wrecv,
+            device_id=(tgx, tgy), device_id_type=MESH,
         ).start()
-        return carry
-
-    lax.fori_loop(1, NX, ask_x, 0)
-    own_x = pltpu.make_async_copy(wq.at[gx], mid.at[gx], loc_sem.at[0])
-    own_x.start()
-
-    others_x = mid.at[pl.ds(0, NX - 1)]
-    others_y = req.at[:, pl.ds(0, NY - 1)]
-
-    def ask_y(k, carry):
-        pltpu.make_async_remote_copy(
-            mid.at[:, other_y(k)], req.at[:, gy], vsend, vrecv,
-            device_id=(gx, other_y(k)), device_id_type=MESH,
-        ).start()
-        return carry
+
+    to_peers(ask)
+    own_ask = pltpu.make_async_copy(wq.at[me], req.at[me], loc_sem.at[0])
+    own_ask.start()
+    others = req.at[pl.ds(0, ND - 1)]
 
     def copy_to(src, dst, send, recv, dgx, dgy):
         return pltpu.make_async_remote_copy(
@@ -388,7 +370,7 @@
             found = peers.block(b, with_self=True)
             for part in range(2):
                 asked = [
-                    jnp.broadcast_to(req[tgx, tgy], (8, 128))
+                    jnp.broadcast_to(req[tgx * NY + tgy], (8, 128))
                     for tgx, tgy, _, _ in found[part * 16 : part * 16 + 16]
                 ]
                 asked = jnp.where(k_mask, jnp.concatenate(asked, axis=0), 0.0)
@@ -469,17 +451,12 @@
     transposed(qrow, place_t)
     placing()
     grid[...] = jnp.zeros_like(grid)
-    own_x.wait()
-    pltpu.make_async_copy(others_x, others_x, wrecv).wait()
-    lax.fori_loop(1, NY, ask_y, 0)
-    own_y = pltpu.make_async_copy(mid.at[:, gy], req.at[:, gy], loc_sem.at[0])
-    own_y.start()
     for h in range(NH):
         take_halo(h, halo_copies[h])
         dynamics(h)
         if h == 0:
-            own_y.wait()
-            pltpu.make_async_copy(others_y, others_y, vrecv).wait()
+            own_ask.wait()
+            pltpu.make_async_copy(others, others, wrecv).wait()
             selections()
         forward[h] = permute_and_send(sel, cols, outb, incb, h, fsend, frecv, 1 + h)
 
@@ -584,8 +561,7 @@
         finish(h)
 
 
-    pltpu.make_async_copy(others_x, others_x, wsend).wait()
-    pltpu.make_async_copy(others_y, others_y, vsend).wait()
+    pltpu.make_async_copy(others, others, wsend).wait()
     for h in range(NH):
         wait_all(outb, h, fsend)
         wait_all(backb, h, bsend)
@@ -645,9 +621,8 @@
     scratch = [
         vmem((4, NHALO * 16, LEV), F32),
         vmem((128, 128), F32),
-        vmem((NX, NY, 1, 128), F32),
-        vmem((NX, NY, 1, 128), F32),
-        vmem((NX, NY, 1, 128), F32),
+        vmem((ND, 1, 128), F32),
+        vmem((ND, 1, 128), F32),
         vmem((8, 128), F32),
         vmem((8, 128), F32),
         vmem((NC, NC), BF16),
@@ -677,7 +652,7 @@
         vmem((NH, 2, 2, 64, LEV), F32),
         vmem((NH, 2, 2, 64, LEV), F32),
         vmem((NH, 4, 8, LEV), F32),
-        dma, dma, dma, dma, dma((5,)),
+        dma, dma, dma((5,)),
         dma((NH,)), dma((NH,)), dma((NH,)), dma((NH,)),
         dma((NH, 8)), dma((NH, 8)), dma((NH, 8)), dma((NH, 8)),
     ]

time: 75.4 us -> 78 us (1.034)
  Pallas kernels: 73.3 us -> 76.1 us
    pallas_call x1, Pallas kernels: 63.4 us -> 66.3 us  [per_device(): pl.pallas_call(exchange_kernel, out_shape=whole, in_specs=[vmem_spec()] *...]
where the time goes in v7:
time: 78 us; the launch traced here: 77.8 us
  Pallas kernels  76.1 us (98%)
  local copies, waits for them, and re-layouts  1.64 us (2%)
    pallas_call x1, Pallas kernels, per_device(): pl.pallas_call(exchange_kernel, out_shape=whole, in_specs=[vmem_spec()] *...  66.3 us
    pallas_call x1, Pallas kernels, per_device(): pl.pallas_call(combine_kernel, out_shape=whole, in_specs=[smem_spec(), an...  6.13 us
    pallas_call x1, Pallas kernels, per_device(): pl.pallas_call(place_kernel, out_shape=jax.ShapeDtypeStruct((4, NE, 16, L...  3.73 us
    unnamed x10, local copies, waits for them, and re-layouts  1.64 us

profile of v7, /device:TPU:1, one launch (start us, length us, event | category | flops | bytes accessed | tf_op | source)
XLA Modules:
  0.0 77.8 jit_solution(5750912116457295917)
XLA Ops:
  0.0 0.0 copy-start.2
  0.0 0.9 %copy-done.2 = f32[16,16,256]{2,1,0:T(8,128)S(1)} copy-done((f32[16,16,256]{2,1,0:T(8,128)S(1)}, f32[16,16,256]{2,1,0:T(8,128)}, u32[]{:S(2)}) %copy-start.2) | copy-done | bytes 262168
  1.0 0.0 copy-start.3
  1.0 0.7 copy-done.3
  1.6 0.0 copy-start
  1.6 0.0 copy-start.1
  1.6 0.0 copy-start.4
  1.6 6.1 %combine.1.st = f32[4,4096,128]{2,1,0:T(8,128)S(1)} custom-call(s32[256]{0:T(256)S(1)} %copy-done.3, f32[4,4096,128]{2,1,0:T(8,128)} %bitcast.9, f32[256,256]{1,0:T(8,128)S(1)} %bitcast.6), custom_call_target="tpu_custom_call" | custom-call | tf_op jit(solution)/shard_map/combine/pallas_call | solution.py:606
  7.8 0.0 copy-done
  7.8 0.0 copy-done.1
  7.8 0.0 copy-done.4
  7.8 66.3 %exchange.1 = f32[4,4096,128]{2,1,0:T(8,128)S(1)} custom-call(f32[4,4096,128]{2,1,0:T(8,128)S(1)} %combine.1.st, s32[2,128]{1,0:T(2,128)S(1)} %bitcast.7, s32[8,128]{1,0:T(8,128)S(1)} %bitcast.8, bf16[64,128,128]{2,1,0:T(8,128)(2,1)S(1)} %copy-done, bf16[640,256]{1,0:T(8,128)(2,1)S(1)} %copy-done.1), custom_call_target="tpu_custom_call" | custom-call | tf_op jit(solution)/shard_map/exchange/pallas_call | solution.py:659
  74.1 3.7 %place.1 = f32[4,256,16,128]{3,2,1,0:T(8,128)} custom-call(s32[256]{0:T(256)S(1)} %copy-done.3, f32[4,256,16,128]{3,2,1,0:T(8,128)S(1)} %bitcast.5), custom_call_target="tpu_custom_call" | custom-call | tf_op jit(solution)/shard_map/place/pallas_call | solution.py:670
Async XLA Ops:
  0.0 0.9 %copy-start.2 = (f32[16,16,256]{2,1,0:T(8,128)S(1)}, f32[16,16,256]{2,1,0:T(8,128)}, u32[]{:S(2)}) copy-start(f32[16,16,256]{2,1,0:T(8,128)} %param.7) | copy-start | bytes 786436
  1.0 0.7 copy-start.3
  1.6 6.1 %copy-start = (bf16[64,128,128]{2,1,0:T(8,128)(2,1)S(1)}, bf16[64,128,128]{2,1,0:T(8,128)(2,1)}, u32[]{:S(2)}) copy-start(bf16[64,128,128]{2,1,0:T(8,128)(2,1)} %inv.1) | copy-start | bytes 6291460
  1.6 6.2 %copy-start.1 = (bf16[640,256]{1,0:T(8,128)(2,1)S(1)}, bf16[640,256]{1,0:T(8,128)(2,1)}, u32[]{:S(2)}) copy-start(bf16[640,256]{1,0:T(8,128)(2,1)} %constant.2.clone.table_ref) | copy-start | bytes 983044
  1.6 6.2 %copy-start.4 = (s32[1024]{0:T(1024)S(1)}, s32[1024]{0:T(1024)}, u32[]{:S(2)}) copy-start(s32[1024]{0:T(1024)} %param.9) | copy-start | bytes 12292
